TPU v7x, 256 devices: a whole 4x4x8 slice. The times are simulated.
256 devices in a mesh: section: 16 (over x, y), ctx: 16 (over z, core).
Axes of the slice: x: 4, y: 4, z: 8, core: 2. Of those that a mesh axis runs over, the one named last changes fastest.
Arguments:
- queries: bfloat16 [2, 16, 2048, 1024], P(None, 'section', 'ctx'), may hold values from -8 to 8
- out_grad: bfloat16 [2, 16, 2048, 1024], P(None, 'section', 'ctx'), may hold values from -6 to 6
- keys: bfloat16 [16, 2048, 128], P('section', 'ctx'), may hold values from -4 to 4
- values: bfloat16 [16, 2048, 128], P('section', 'ctx'), may hold values from -6 to 6
- entering_keys: bfloat16 [2048, 128], P('ctx'), may hold values from -4 to 4
- entering_values: bfloat16 [2048, 128], P('ctx'), may hold values from -6 to 6
- key_grads_in: float32 [16, 2048, 128], P('section', 'ctx'), may hold values from -4 to 4
- value_grads_in: float32 [16, 2048, 128], P('section', 'ctx'), may hold values from -4 to 4
- group_order: int32 [16], replicated, may hold values from 0 to 15, each once
Outputs:
- query_grads: bfloat16 [2, 16, 2048, 1024], P(None, 'section', 'ctx')
- key_grads: float32 [2, 16, 2048, 128], P(None, 'section', 'ctx')
- value_grads: float32 [2, 16, 2048, 128], P(None, 'section', 'ctx')
Inputs may be any that keep to these rules, and one draw needn't show every extreme that they name: `group_order`: each number 0 to 15 appears once.
All inputs are finite; a program needn't handle non-finite values.
Results may differ from a plain program's by a relative error of at most 0.0062.
Values may be sent and summed in bfloat16 or wider, within the bound.
A program may use at most 128 MiB of HBM per device.

v0:
```python
import math

import jax
import jax.numpy as jnp
from jax import lax
from jax.sharding import PartitionSpec as P

HEADS = 8


MASK_FILL = -1e30


def copy_for_each(array, axis):
    copies = jnp.broadcast_to(array, (lax.axis_size(axis), *array.shape))
    return lax.all_to_all(copies, axis, split_axis=0, concat_axis=0, tiled=True)


def joined_along(parts, dim):
    dims = list(parts.shape[1:])
    dims[dim] *= parts.shape[0]
    return jnp.moveaxis(parts, 0, dim).reshape(dims)


def collect(array, axis, dim):
    parts = copy_for_each(array, axis)
    return joined_along(parts, dim)


def split_up(array, dim, peers):
    before, after = (array.shape[:dim], array.shape[dim + 1 :])
    return jnp.moveaxis(array.reshape(*before, peers, -1, *after), dim, 0)


def sum_at_owner(array, axis, dim):
    peers = lax.axis_size(axis)
    parts = lax.all_to_all(split_up(array, dim, peers), axis, 0, 0, tiled=True)
    return jnp.sum(parts, axis=0)


def shifted(block, axis, distance):
    devices = range(lax.axis_size(axis))
    route = [(i - distance, i) for i in devices if i - distance in devices]
    return lax.ppermute(block, axis, route)


def body(
    queries,
    out_grad,
    keys,
    values,
    entering_keys,
    entering_values,
    key_grads_in,
    value_grads_in,
    group_order,
):
    local_rows = keys.shape[1]
    head_dim = keys.shape[2]
    ctx_count = lax.axis_size("ctx")
    score_scale = 1.0 / math.sqrt(head_dim)
    ctx_index = lax.axis_index("ctx")
    slot_ids = jnp.arange(ctx_count, dtype=jnp.int32)
    own_group = jnp.sum(jnp.where(slot_ids == ctx_index, group_order, 0))
    query_pos = own_group * local_rows + jnp.arange(local_rows, dtype=jnp.int32)
    query_rows = jnp.repeat(query_pos, HEADS)
    flat_rows = local_rows * HEADS

    def key_positions(row_count):
        row_ids = jnp.arange(row_count, dtype=jnp.int32)
        shard_ids = row_ids // local_rows
        group_ids = jnp.sum(
            jnp.where(shard_ids[:, None] == slot_ids[None, :], group_order[None, :], 0), axis=1
        )
        return group_ids * local_rows + row_ids % local_rows

    def one_tick(query_block, grad_block, kv_pair, carried):
        queries_flat = query_block.reshape(flat_rows, head_dim)
        grads_flat = grad_block.reshape(flat_rows, head_dim)
        whole = collect(kv_pair, "ctx", 0)
        key_block = whole[:, :head_dim]
        value_block = whole[:, head_dim:]
        allowed = key_positions(whole.shape[0])[None, :] <= query_rows[:, None]
        raw = (
            jnp.dot(queries_flat, whole[:, :head_dim].T, preferred_element_type=jnp.float32)
            * score_scale
        )
        scores = jnp.where(allowed, raw, MASK_FILL)
        biggest = jnp.max(scores, axis=1, keepdims=True)
        expo = jnp.where(allowed, jnp.exp(scores - biggest), 0.0)
        probs = expo / jnp.sum(expo, axis=1, keepdims=True)
        prob_grads = jnp.dot(grads_flat, value_block.T, preferred_element_type=jnp.float32)
        deltas = jnp.sum(probs * prob_grads, axis=1, keepdims=True)
        score_grad = (probs * (prob_grads - deltas)).astype(jnp.bfloat16)
        probs_half = probs.astype(jnp.bfloat16)
        query_sum = jnp.dot(score_grad, key_block, preferred_element_type=jnp.float32)
        key_terms = (
            jnp.dot(score_grad.T, queries_flat, preferred_element_type=jnp.float32) * score_scale
        )
        value_terms = jnp.dot(probs_half.T, grads_flat, preferred_element_type=jnp.float32)
        terms = jnp.concatenate([key_terms, value_terms], axis=1)
        query_grad = (
            (query_sum * score_scale).astype(jnp.bfloat16).reshape(local_rows, HEADS * head_dim)
        )
        summed = sum_at_owner(terms, "ctx", 0)
        return (query_grad, carried + summed)

    first_pair = jnp.concatenate([keys[0], values[0]], axis=1)
    first_carried = jnp.concatenate([key_grads_in[0], value_grads_in[0]], axis=1)
    first_query, first_acc = one_tick(queries[0, 0], out_grad[0, 0], first_pair, first_carried)
    moved_pair = shifted(first_pair, "section", -1)
    moved_acc = shifted(first_acc, "section", -1)
    is_last = lax.axis_index("section") == lax.axis_size("section") - 1
    entering_pair = jnp.concatenate([entering_keys, entering_values], axis=1)
    second_pair = jnp.where(is_last, entering_pair, moved_pair)
    second_query, second_acc = one_tick(queries[1, 0], out_grad[1, 0], second_pair, moved_acc)
    query_grads = jnp.stack([first_query, second_query], axis=0)[:, None]
    key_grads = jnp.stack([first_acc[:, :head_dim], second_acc[:, :head_dim]], axis=0)[:, None]
    value_grads = jnp.stack([first_acc[:, head_dim:], second_acc[:, head_dim:]], axis=0)[:, None]
    return (query_grads, key_grads, value_grads)


def solution(mesh):
    return jax.shard_map(
        body,
        mesh=mesh,
        in_specs=(
            P(None, "section", "ctx", None),
            P(None, "section", "ctx", None),
            P("section", "ctx", None),
            P("section", "ctx", None),
            P("ctx", None),
            P("ctx", None),
            P("section", "ctx", None),
            P("section", "ctx", None),
            P(),
        ),
        out_specs=(
            P(None, "section", "ctx", None),
            P(None, "section", "ctx", None),
            P(None, "section", "ctx", None),
        ),
        check_vma=False,
    )
```

profile of v0, /device:TPU:1, one launch (start us, length us, event | category | flops | bytes accessed | tf_op | source)
XLA Modules:
  0.0 221.4 jit_solution(17533677255843409192)
XLA Ops:
  2.5 10.0 %all-to-all-start = ((bf16[16,128,256]{2,1,0:T(8,128)(2,1)}), bf16[16,128,256]{2,1,0:T(8,128)(2,1)S(1)}, u32[]{:S(2)}, u32[]{:S(2)}) async-start(bf16[16,128,256]{2,1,0:T(8,128)(2,1)} %broadcast_in_dim.65), calls=%async_computation | async-start | bytes 2097152 | tf_op jit(solution)/shard_map/all_to_all | solution.py:16
  13.8 4.1 %collective-permute-done = bf16[128,256]{1,0:T(8,128)(2,1)S(1)} collective-permute-done((bf16[128,256]{1,0:T(8,128)(2,1)S(1)}, bf16[128,256]{1,0:T(8,128)(2,1)S(1)}, u32[]{:S(2)}, u32[]{:S(2)}) %collective-permute-start) | collective-permute-done | bytes 65568 | tf_op jit(solution)/shard_map/ppermute | solution.py:44
  18.7 21.8 %all-to-all-done = bf16[16,128,256]{2,1,0:T(8,128)(2,1)S(1)} async-done(((bf16[16,128,256]{2,1,0:T(8,128)(2,1)}), bf16[16,128,256]{2,1,0:T(8,128)(2,1)S(1)}, u32[]{:S(2)}, u32[]{:S(2)}) %all-to-all-start) | async-done | bytes 1048608 | tf_op jit(solution)/shard_map/all_to_all | solution.py:16
  41.5 3.5 %all-to-all-start.1 = ((bf16[16,128,256]{2,1,0:T(8,128)(2,1)}), bf16[16,128,256]{2,1,0:T(8,128)(2,1)S(1)}, u32[]{:S(2)}, u32[]{:S(2)}) async-start(bf16[16,128,256]{2,1,0:T(8,128)(2,1)} %broadcast_in_dim.68), calls=%async_computation.1 | async-start | bytes 2097152 | tf_op jit(solution)/shard_map/all_to_all | solution.py:16
  51.4 4.0 %fusion.6 = (f32[1024]{0:T(1024)S(1)}, f32[2048,1024]{1,0:T(8,128)}) fusion(s32[1024]{0:T(1024)S(1)} %le.9, s32[2048]{0:T(1024)S(1)} %fusion.34, bf16[1024,128]{1,0:T(8,128)(2,1)S(1)} %reshape_squeeze.12, bf16[2048,256]{1,0:T(8,128)(2,1)S(1)} %bitcast.102), kind=kOutput, calls=%fused_computation.14 | convolution fusion | flops 545258496 | bytes 9191424 | tf_op jit(solution)/shard_map/dot_general | solution.py:85
  55.4 17.6 %all-to-all-done.1 = bf16[16,128,256]{2,1,0:T(8,128)(2,1)S(1)} async-done(((bf16[16,128,256]{2,1,0:T(8,128)(2,1)}), bf16[16,128,256]{2,1,0:T(8,128)(2,1)S(1)}, u32[]{:S(2)}, u32[]{:S(2)}) %all-to-all-start.1) | async-done | bytes 1048608 | tf_op jit(solution)/shard_map/all_to_all | solution.py:16
  73.0 7.5 %fusion.9 = (f32[1024]{0:T(1024)S(1)}, f32[1024]{0:T(1024)S(1)}, f32[2048,1024]{1,0:T(8,128)S(1)}) fusion(f32[2048,1024]{1,0:T(8,128)} %get-tuple-element.24, f32[1024]{0:T(1024)S(1)} %get-tuple-element.23, s32[1024]{0:T(1024)S(1)} %le.9, s32[2048]{0:T(1024)S(1)} %fusion.34, bf16[1024,128]{1,0:T(8,128)(2,1)S(1)} %reshape_squeeze.14, ...), kind=kOutput, calls=%fused_computation.17 | convolution fusion | flops 555743232 | bytes 17588224 | tf_op jit(solution)/shard_map/dot_general | solution.py:85
  80.6 2.6 %fusion.14 = f32[2048,128]{0,1:T(8,128)S(1)} fusion(bf16[1024,128]{1,0:T(8,128)(2,1)S(1)} %copy-done.7, f32[2048,1024]{1,0:T(8,128)S(1)} %copy-done.2, f32[1024]{0:T(1024)S(1)} %get-tuple-element.11, f32[1024]{0:T(1024)S(1)} %get-tuple-element.23, s32[1024]{0:T(1024)S(1)} %le.9, s32[2048]{0:T(1024)S(1)} %fusion.34), kind=kOutput, calls=%fused_computation.22 | convolution fusion | flops 551550976 | bytes 9719808 | tf_op jit(solution)/shard_map/dot_general | solution.py:100
  83.2 6.8 %fusion.3 = (f32[1024]{0:T(1024)S(1)}, f32[1024]{0:T(1024)S(1)}, f32[2048,1024]{1,0:T(8,128)}) fusion(f32[1024]{0:T(1024)S(1)} %get-tuple-element.11, f32[1024]{0:T(1024)S(1)} %get-tuple-element.23, f32[2048,1024]{1,0:T(8,128)S(1)} %copy-done.2, s32[1024]{0:T(1024)S(1)} %le.9, s32[2048]{0:T(1024)S(1)} %fusion.34, f32[1024]{0:T(1024)S(1)} %get-tuple-element.12, ...), kind=kOutput, calls=%fused_computation.11 | convolution fusion | flops 564131840 | bytes 25985024 | tf_op jit(solution)/shard_map/dot_general | solution.py:92
  90.0 5.4 %fusion = (f32[1024]{0:T(1024)S(1)}, f32[2048,1024]{1,0:T(8,128)}) fusion(f32[1024]{0:T(1024)S(1)} %get-tuple-element.10, f32[1024]{0:T(1024)S(1)} %get-tuple-element.12, f32[2048,1024]{1,0:T(8,128)S(1)} %get-tuple-element.25, s32[1024]{0:T(1024)S(1)} %le.9, s32[2048]{0:T(1024)S(1)} %fusion.34, bf16[1024,128]{1,0:T(8,128)(2,1)S(1)} %copy-done.6, ...), kind=kOutput, calls=%fused_computation.6 | convolution fusion | flops 553647104 | bytes 17588224 | tf_op jit(solution)/shard_map/dot_general | solution.py:92
  95.4 11.2 %fusion.5 = (bf16[1024,2048]{0,1:T(8,128)(2,1)S(1)}, bf16[1024,2048]{0,1:T(8,128)(2,1)}) fusion(f32[2048,1024]{1,0:T(8,128)} %get-tuple-element.26, f32[1024]{0:T(1024)S(1)} %get-tuple-element.9, f32[1024]{0:T(1024)S(1)} %get-tuple-element.11, f32[1024]{0:T(1024)S(1)} %get-tuple-element.23, f32[2048,1024]{1,0:T(8,128)S(1)} %copy-done.2, s32[1024]{0:T(1024)S(1)} %le.9, ...), kind=kLoop, calls=%fused_computation.13 | loop fusion | flops 35651584 | bytes 41979904 | tf_op jit(solution)/shard_map/convert_element_type | solution.py:94
  106.6 2.0 copy-done
  108.6 1.5 convolution_multiply_fusion.1
  110.1 1.5 copy_bitcast_fusion.1
  111.6 3.8 %all-to-all-start.2 = ((f32[16,128,256]{1,2,0:T(8,128)}), f32[16,128,256]{1,2,0:T(8,128)S(1)}, u32[]{:S(2)}, u32[]{:S(2)}) async-start(f32[16,128,256]{1,2,0:T(8,128)} %copy_bitcast_fusion.1), calls=%async_computation.2 | async-start | bytes 4194304 | tf_op jit(solution)/shard_map/all_to_all | solution.py:37
  115.4 3.7 %convolution_multiply_fusion = f32[2048,128]{0,1:T(8,128)S(1)} fusion(bf16[1024,2048]{0,1:T(8,128)(2,1)} %get-tuple-element.22, bf16[1024,128]{1,0:T(8,128)(2,1)S(1)} %reshape_squeeze.14), kind=kOutput, calls=%fused_computation.24 | convolution fusion | flops 537133056 | bytes 5505024 | tf_op jit(solution)/shard_map/dot_general | solution.py:98
  119.2 5.2 %fusion.12 = f32[2048,128]{0,1:T(8,128)S(1)} fusion(bf16[1024,128]{1,0:T(8,128)(2,1)} %reshape_squeeze.15, f32[2048,1024]{1,0:T(8,128)} %copy-done.1, f32[1024]{0:T(1024)S(1)} %get-tuple-element.10, f32[1024]{0:T(1024)S(1)} %get-tuple-element.12, s32[1024]{0:T(1024)S(1)} %le.9, s32[2048]{0:T(1024)S(1)} %fusion.34), kind=kOutput, calls=%fused_computation.20 | convolution fusion | flops 551550976 | bytes 9719808 | tf_op jit(solution)/shard_map/dot_general | solution.py:100
  124.4 1.6 copy_bitcast_fusion
  125.9 38.2 %all-to-all-done.2 = f32[16,128,256]{1,2,0:T(8,128)S(1)} async-done(((f32[16,128,256]{1,2,0:T(8,128)}), f32[16,128,256]{1,2,0:T(8,128)S(1)}, u32[]{:S(2)}, u32[]{:S(2)}) %all-to-all-start.2) | async-done | bytes 2097184 | tf_op jit(solution)/shard_map/all_to_all | solution.py:37
  164.1 4.9 %all-to-all-start.3 = ((f32[16,128,256]{1,2,0:T(8,128)}), f32[16,128,256]{1,2,0:T(8,128)}, u32[]{:S(2)}, u32[]{:S(2)}) async-start(f32[16,128,256]{1,2,0:T(8,128)} %copy_bitcast_fusion), calls=%async_computation.3 | async-start | bytes 4194304 | tf_op jit(solution)/shard_map/all_to_all | solution.py:37
  169.2 4.3 %fusion.17 = bf16[1024,128]{1,0:T(8,128)(2,1)} fusion(bf16[1024,2048]{0,1:T(8,128)(2,1)} %get-tuple-element.22, bf16[2048,256]{1,0:T(8,128)(2,1)} %bitcast.107), kind=kOutput, calls=%fused_computation.33 | convolution fusion | flops 537133056 | bytes 4980736 | tf_op jit(solution)/shard_map/dot_general | solution.py:96
  174.6 4.2 %fusion.16 = bf16[1024,128]{1,0:T(8,128)(2,1)} fusion(bf16[1024,2048]{0,1:T(8,128)(2,1)} %copy-done, bf16[2048,256]{1,0:T(8,128)(2,1)S(1)} %bitcast.104), kind=kOutput, calls=%fused_computation.32 | convolution fusion | flops 537133056 | bytes 4980736 | tf_op jit(solution)/shard_map/dot_general | solution.py:96
  182.1 36.0 %all-to-all-done.3 = f32[16,128,256]{1,2,0:T(8,128)} async-done(((f32[16,128,256]{1,2,0:T(8,128)}), f32[16,128,256]{1,2,0:T(8,128)}, u32[]{:S(2)}, u32[]{:S(2)}) %all-to-all-start.3) | async-done | bytes 2097184 | tf_op jit(solution)/shard_map/all_to_all | solution.py:37
  218.1 1.7 reduce_sum.83
  (54 shorter events, 16.8 us)
Async XLA Ops:
  0.6 50.7 %copy-start.10 = (s32[16]{0:T(128)S(1)}, s32[16]{0:T(128)}, u32[]{:S(2)}) copy-start(s32[16]{0:T(128)} %param.17) | copy-start | bytes 196
  2.5 38.0 %all-to-all-start = ((bf16[16,128,256]{2,1,0:T(8,128)(2,1)}), bf16[16,128,256]{2,1,0:T(8,128)(2,1)S(1)}, u32[]{:S(2)}, u32[]{:S(2)}) async-start(bf16[16,128,256]{2,1,0:T(8,128)(2,1)} %broadcast_in_dim.65), calls=%async_computation | async-start | bytes 2097152 | tf_op jit(solution)/shard_map/all_to_all | solution.py:16
  12.5 5.4 %collective-permute-start = (bf16[128,256]{1,0:T(8,128)(2,1)S(1)}, bf16[128,256]{1,0:T(8,128)(2,1)S(1)}, u32[]{:S(2)}, u32[]{:S(2)}) collective-permute-start(bf16[128,256]{1,0:T(8,128)(2,1)S(1)} %pad_maximum_fusion), channel_id=1, source_target_pairs={{16,0},{32,16},{48,32},{64,48},{80,64},{96,80},{112,96},{128,112},... | collective-permute-start | bytes 196616 | tf_op jit(solution)/shard_map/ppermute | solution.py:44
  41.5 31.4 %all-to-all-start.1 = ((bf16[16,128,256]{2,1,0:T(8,128)(2,1)}), bf16[16,128,256]{2,1,0:T(8,128)(2,1)S(1)}, u32[]{:S(2)}, u32[]{:S(2)}) async-start(bf16[16,128,256]{2,1,0:T(8,128)(2,1)} %broadcast_in_dim.68), calls=%async_computation.1 | async-start | bytes 2097152 | tf_op jit(solution)/shard_map/all_to_all | solution.py:16
  48.4 6.9 %copy-start.4 = (bf16[1024,128]{1,0:T(8,128)(2,1)}, bf16[1024,128]{1,0:T(8,128)(2,1)S(1)}, u32[]{:S(2)}) copy-start(bf16[1024,128]{1,0:T(8,128)(2,1)S(1)} %reshape_squeeze.12) | copy-start | bytes 786436
  73.0 17.0 %copy-start.3 = (bf16[16,128,256]{2,1,0:T(8,128)(2,1)}, bf16[16,128,256]{2,1,0:T(8,128)(2,1)S(1)}, u32[]{:S(2)}) copy-start(bf16[16,128,256]{2,1,0:T(8,128)(2,1)S(1)} %all-to-all-done.1) | copy-start | bytes 3145732
  73.0 7.6 %copy-start.2 = (f32[2048,1024]{1,0:T(8,128)S(1)}, f32[2048,1024]{1,0:T(8,128)}, u32[]{:S(2)}) copy-start(f32[2048,1024]{1,0:T(8,128)} %get-tuple-element.24) | copy-start | bytes 25165828
  73.0 7.6 %copy-start.7 = (bf16[1024,128]{1,0:T(8,128)(2,1)S(1)}, bf16[1024,128]{1,0:T(8,128)(2,1)}, u32[]{:S(2)}) copy-start(bf16[1024,128]{1,0:T(8,128)(2,1)} %reshape_squeeze.13) | copy-start | bytes 786436
  80.5 14.8 %copy-start.1 = (f32[2048,1024]{1,0:T(8,128)}, f32[2048,1024]{1,0:T(8,128)S(1)}, u32[]{:S(2)}) copy-start(f32[2048,1024]{1,0:T(8,128)S(1)} %get-tuple-element.25) | copy-start | bytes 25165828
  83.2 6.8 %copy-start.6 = (bf16[1024,128]{1,0:T(8,128)(2,1)S(1)}, bf16[1024,128]{1,0:T(8,128)(2,1)}, u32[]{:S(2)}) copy-start(bf16[1024,128]{1,0:T(8,128)(2,1)} %reshape_squeeze.15) | copy-start | bytes 786436
  95.4 13.2 %copy-start.5 = (bf16[1024,128]{1,0:T(8,128)(2,1)S(1)}, bf16[1024,128]{1,0:T(8,128)(2,1)}, u32[]{:S(2)}) copy-start(bf16[1024,128]{1,0:T(8,128)(2,1)} %copy-done.4) | copy-start | bytes 786436
  106.6 2.0 copy-start
  111.6 52.4 %all-to-all-start.2 = ((f32[16,128,256]{1,2,0:T(8,128)}), f32[16,128,256]{1,2,0:T(8,128)S(1)}, u32[]{:S(2)}, u32[]{:S(2)}) async-start(f32[16,128,256]{1,2,0:T(8,128)} %copy_bitcast_fusion.1), calls=%async_computation.2 | async-start | bytes 4194304 | tf_op jit(solution)/shard_map/all_to_all | solution.py:37
  124.3 44.6 %copy-start.8 = (f32[1,128,128]{2,1,0:T(8,128)S(1)}, f32[1,128,128]{2,1,0:T(8,128)}, u32[]{:S(2)}) copy-start(f32[1,128,128]{2,1,0:T(8,128)} %param.16) | copy-start | bytes 196612
  124.4 44.7 %copy-start.9 = (f32[1,128,128]{2,1,0:T(8,128)S(1)}, f32[1,128,128]{2,1,0:T(8,128)}, u32[]{:S(2)}) copy-start(f32[1,128,128]{2,1,0:T(8,128)} %param.15) | copy-start | bytes 196612
  164.1 54.1 %all-to-all-start.3 = ((f32[16,128,256]{1,2,0:T(8,128)}), f32[16,128,256]{1,2,0:T(8,128)}, u32[]{:S(2)}, u32[]{:S(2)}) async-start(f32[16,128,256]{1,2,0:T(8,128)} %copy_bitcast_fusion), calls=%async_computation.3 | async-start | bytes 4194304 | tf_op jit(solution)/shard_map/all_to_all | solution.py:37
  180.8 39.1 %collective-permute-start.1 = (f32[128,256]{0,1:T(8,128)S(1)}, f32[128,256]{0,1:T(8,128)S(1)}, u32[]{:S(2)}, u32[]{:S(2)}) collective-permute-start(f32[128,256]{0,1:T(8,128)S(1)} %maximum_add_fusion), channel_id=1, source_target_pairs={{16,0},{32,16},{48,32},{64,48},{80,64},{96,80},{112,96},{128,112},... | collective-permute-start | bytes 393224 | tf_op jit(solution)/shard_map/ppermute | solution.py:44
where the time goes:
time: 222 us; the launch traced here: 221 us
  waiting for transfers between devices  118 us (53%)
  matrix products  45.2 us (20%)
  starting transfers between devices  24.8 us (11%)
  other arithmetic  20 us (9%)
  local copies, waits for them, and re-layouts  12.2 us (5%)
    all_to_all x2, waiting for transfers between devices, sum_at_owner(): parts = lax.all_to_all(split_up(array, dim, peers), axis, 0, 0, tiled=True)  74.2 us
    all_to_all x2, waiting for transfers between devices, copy_for_each(): return lax.all_to_all(copies, axis, split_axis=0, concat_axis=0, tiled=True)  39.4 us
    all_to_all x2, starting transfers between devices, copy_for_each(): return lax.all_to_all(copies, axis, split_axis=0, concat_axis=0, tiled=True)  13.5 us
    dot_general x2, matrix products, one_tick(): jnp.dot(grads_flat, value_block.T, preferred_element_type=jnp.float32)  12.2 us
    dot_general x2, matrix products, one_tick(): jnp.dot(queries_flat, whole[:, :head_dim].T, preferred_element_type=jnp.f...  11.5 us
    convert_element_type x1, other arithmetic, one_tick(): score_grad = (probs * (prob_grads - deltas)).astype(jnp.bfloat16)  11.2 us
    all_to_all x2, starting transfers between devices, sum_at_owner(): parts = lax.all_to_all(split_up(array, dim, peers), axis, 0, 0, tiled=True)  8.7 us
    dot_general x2, matrix products, one_tick(): jnp.dot(score_grad, key_block, preferred_element_type=jnp.float32)  8.51 us
  transfers between devices with their start and end apart: 6, of which 5 were waited for; matrix products, arithmetic and copies ran while one was open for 15% of the time, Pallas kernels for 0%

commit v1 on v0

v1 whole, which is shorter than its diff:
```python
import functools
import math

import jax
import jax.numpy as jnp
from jax import lax
from jax.experimental import pallas as pl
from jax.experimental.pallas import tpu as pltpu
from jax.sharding import PartitionSpec as P

HEADS = 8
DIM = 128
ROWS = 128
CHUNK = 256
WIDE = 512
NEG = -1e30
MESH = pl.DeviceIdType.MESH
SCALE = 1.0 / math.sqrt(DIM)
LOG2E = 1.4426950408889634
NT = (((1,), (1,)), ((), ()))
NN = (((1,), (0,)), ((), ()))


def mm(a, b, dims=NN):
    return lax.dot_general(a, b, dims, preferred_element_type=jnp.float32)


def offsets_of(chips):
    out = [0]
    for d in range(1, chips // 2):
        out += [d, -d]
    return out + [chips // 2]


def kernel(
    chips,
    sections,
    order_ref,
    q_ref,
    g_ref,
    k_ref,
    v_ref,
    ek_ref,
    ev_ref,
    ka_ref,
    va_ref,
    dq_ref,
    dk_ref,
    dv_ref,
    qb,
    gb,
    kb,
    vb,
    kt,
    eb,
    db,
    mst,
    lst,
    dsum,
    fst,
    st_out,
    st_in,
    pbuf,
    sbuf,
    acc,
    dqt,
    dq_in,
    rs_out,
    rs_in,
    acc_own,
    acc_in,
    load_sem,
    kv_sem,
    xs,
    xr,
    ags,
    agr,
    sts,
    stv,
    dqs,
    dqr,
    rss,
    rsr,
    cs,
    cr,
    acc_sem,
):
    offsets = offsets_of(chips)
    split = [(0, 3), (3, 5), (5, 8)] if chips == 8 else [(0, 3), (3, 4)]
    sec = lax.axis_index("section")
    cx = lax.axis_index("ctx")
    chip = cx // 2
    core = lax.rem(cx, 2)
    prev = lax.rem(sec + sections - 1, sections)
    nxt = lax.rem(sec + 1, sections)
    partner = (sec, chip * 2 + 1 - core)

    def peer(section, offset):
        return (section, lax.rem(chip + offset + chips, chips) * 2 + core)

    barrier = pltpu.get_barrier_semaphore()
    for off in offsets[1:]:
        pl.semaphore_signal(barrier, inc=1, device_id=peer(sec, off), device_id_type=MESH)
    pl.semaphore_signal(barrier, inc=1, device_id=partner, device_id_type=MESH)
    for off in offsets:
        pl.semaphore_signal(barrier, inc=1, device_id=peer(nxt, off), device_id_type=MESH)
        pl.semaphore_signal(barrier, inc=1, device_id=peer(prev, off), device_id_type=MESH)

    def local(src, dst, sem):
        return pltpu.make_async_copy(src, dst, sem)

    def remote(src, dst, s, r, dev):
        return pltpu.make_async_remote_copy(
            src_ref=src, dst_ref=dst, send_sem=s, recv_sem=r, device_id=dev, device_id_type=MESH
        )

    own_kv = [
        local(k_ref.at[0], kb.at[0, pl.ds(0, ROWS)], kv_sem.at[0]),
        local(v_ref.at[0], vb.at[0, pl.ds(0, ROWS)], kv_sem.at[1]),
    ]
    loads = []
    for t in range(2):
        for i, (src, dst) in enumerate(((q_ref, qb), (g_ref, gb))):
            for h in range(HEADS):
                loads.append(
                    local(
                        src.at[t, 0, :, pl.ds(h * DIM, DIM)],
                        dst.at[t, core, h],
                        load_sem.at[t, i, h],
                    )
                )
    acc_loads = [
        local(ka_ref.at[0], acc_in.at[0, 0], acc_sem.at[0]),
        local(va_ref.at[0], acc_in.at[0, 1], acc_sem.at[1]),
    ]
    for cp in own_kv + loads + acc_loads:
        cp.start()

    pl.semaphore_wait(barrier, (chips - 1) + 1 + 2 * chips)

    gather = [[], []]
    for p in range(1, chips):
        dev = peer(sec, offsets[p])
        rows = pl.ds(p * ROWS, ROWS)
        gather[0].append(remote(k_ref.at[0], kb.at[0, rows], ags.at[0, p, 0], agr.at[0, p, 0], dev))
        gather[0].append(remote(v_ref.at[0], vb.at[0, rows], ags.at[0, p, 1], agr.at[0, p, 1], dev))
    for cp in gather[0]:
        cp.start()

    swaps = [[], []]
    for t in range(2):
        for i, (src, dst) in enumerate(((q_ref, qb), (g_ref, gb))):
            for h in range(HEADS):
                swaps[t].append(
                    remote(
                        src.at[t, 0, :, pl.ds(h * DIM, DIM)],
                        dst.at[t, core, h],
                        xs.at[t, i, h],
                        xr.at[t, i, h],
                        partner,
                    )
                )
    for cp in swaps[0]:
        cp.start()

    def next_gather(k_src, v_src):
        out = []
        for p in range(chips):
            dev = peer(prev, offsets[p])
            rows = pl.ds(p * ROWS, ROWS)
            out.append(remote(k_src, kb.at[1, rows], ags.at[1, p, 0], agr.at[1, p, 0], dev))
            out.append(remote(v_src, vb.at[1, rows], ags.at[1, p, 1], agr.at[1, p, 1], dev))
        return out

    @pl.when(sec > 0)
    def _():
        for cp in next_gather(k_ref.at[0], v_ref.at[0]):
            cp.start()

    @pl.when(sec == 0)
    def _():
        for cp in next_gather(ek_ref, ev_ref):
            cp.start()

    gather[1] = next_gather(k_ref.at[0], v_ref.at[0])
    for cp in swaps[1]:
        cp.start()
    for cp in own_kv + loads + acc_loads:
        cp.wait()

    c_exp = SCALE * LOG2E
    diff = lax.broadcasted_iota(jnp.int32, (ROWS, CHUNK), 0) - lax.rem(
        lax.broadcasted_iota(jnp.int32, (ROWS, CHUNK), 1), ROWS
    )
    total = 2 * HEADS * ROWS

    def key_group(p):
        return order_ref[lax.rem(chip - offsets[p] + chips, chips) * 2 + core]

    def first_pass(t, a, b):
        keys = kb[t, pl.ds(a * ROWS, (b - a) * ROWS), :]
        values = vb[t, pl.ds(a * ROWS, (b - a) * ROWS), :]

        @pl.loop(0, total // CHUNK)
        def _(j):
            half = j // (HEADS // 2)
            pair = pl.ds(lax.rem(j, HEADS // 2) * 2, 2)
            qs = qb[t, half, pair].reshape(CHUNK, DIM)
            gs = gb[t, half, pair].reshape(CHUNK, DIM)
            lanes = pl.ds(pl.multiple_of(j * CHUNK, CHUNK), CHUNK)
            s_all = mm(keys, qs, NT)
            d_all = mm(values, gs, NT)
            query_group = order_ref[chip * 2 + half]
            for p in range(a, b):
                part = slice((p - a) * ROWS, (p - a + 1) * ROWS)
                limit = (query_group - key_group(p)) * ROWS
                s = jnp.where(diff <= limit, s_all[part], NEG)
                m = jnp.max(s, axis=0, keepdims=True)
                e = jnp.exp2((s - m) * c_exp)
                d = d_all[part]
                eb[pl.ds(p * ROWS, ROWS), lanes] = e
                db[pl.ds(p * ROWS, ROWS), lanes] = d
                mst[pl.ds(p, 1), lanes] = m
                lst[pl.ds(p, 1), lanes] = jnp.sum(e, axis=0, keepdims=True)
                dsum[pl.ds(p, 1), lanes] = jnp.sum(e * d, axis=0, keepdims=True)

    def stats(t):
        m_b = mst[...]
        m_own = jnp.max(m_b, axis=0, keepdims=True)
        w = jnp.exp2((m_b - m_own) * c_exp)
        l_own = jnp.sum(lst[...] * w, axis=0, keepdims=True)
        d_own = jnp.sum(dsum[...] * w, axis=0, keepdims=True)
        row = lax.broadcasted_iota(jnp.int32, (8, total), 0)
        st_out[t] = jnp.where(row == 0, m_own, jnp.where(row == 1, l_own, d_own))
        cp = remote(st_out.at[t], st_in.at[t], sts.at[t], stv.at[t], partner)
        cp.start()
        cp.wait()
        m_far = st_in[t, 0:1, :]
        m = jnp.maximum(m_own, m_far)
        w_own = jnp.exp2((m_own - m) * c_exp)
        w_far = jnp.exp2((m_far - m) * c_exp)
        inv = 1.0 / (l_own * w_own + st_in[t, 1:2, :] * w_far)
        delta = (d_own * w_own + st_in[t, 2:3, :] * w_far) * inv
        fst[0] = jnp.exp2((m_b - m) * c_exp) * inv
        fst[1] = jnp.broadcast_to(delta, (chips, total))

    def second_pass(t, a, b, first):
        m_rows = (b - a) * ROWS
        acc[...] = jnp.zeros_like(acc)

        @pl.loop(0, total // WIDE)
        def _(j):
            lanes = pl.ds(pl.multiple_of(j * WIDE, WIDE), WIDE)
            half = j // (HEADS // 4)
            group = pl.ds(lax.rem(j, HEADS // 4) * 4, 4)
            delta = fst[1, 0:1, lanes]
            for p in range(a, b):
                prob = eb[pl.ds(p * ROWS, ROWS), lanes] * fst[0, p : p + 1, lanes]
                ds = prob * (db[pl.ds(p * ROWS, ROWS), lanes] - delta)
                pbuf[pl.ds((p - a) * ROWS, ROWS), :] = prob.astype(jnp.bfloat16)
                sbuf[pl.ds((p - a) * ROWS, ROWS), :] = ds.astype(jnp.bfloat16)
            pr = pbuf[pl.ds(0, m_rows), :]
            sg = sbuf[pl.ds(0, m_rows), :]
            acc[0, pl.ds(0, m_rows), :] += mm(sg, qb[t, half, group].reshape(WIDE, DIM))
            acc[1, pl.ds(0, m_rows), :] += mm(pr, gb[t, half, group].reshape(WIDE, DIM))
            part = mm(kt[:, pl.ds(a * ROWS, m_rows)], sg)
            if first:
                dqt[:, lanes] = part
            else:
                dqt[:, lanes] += part

    def send_terms(t, a, b):
        out = []
        for p in range(a, b):
            rows = pl.ds((p - a) * ROWS, ROWS)
            if p == 0:
                acc_own[t, 0] = acc[0, rows, :] * SCALE
                acc_own[t, 1] = acc[1, rows, :]
            else:
                rs_out[t, p, 0] = (acc[0, rows, :] * SCALE).astype(jnp.bfloat16)
                rs_out[t, p, 1] = acc[1, rows, :].astype(jnp.bfloat16)
                cp = remote(
                    rs_out.at[t, p], rs_in.at[t, p], rss.at[t, p], rsr.at[t, p], peer(sec, -offsets[p])
                )
                cp.start()
                out.append(cp)
        return out

    def finish_queries(t, cp):
        cp.wait()
        for h in range(HEADS):
            own = pl.ds(pl.multiple_of(core * HEADS * ROWS + h * ROWS, ROWS), ROWS)
            full = (dqt[:, own] + dq_in[t, :, pl.ds(h * ROWS, ROWS)]) * SCALE
            dq_ref[t, 0, :, pl.ds(h * DIM, DIM)] = full.T.astype(jnp.bfloat16)

    def finish_terms(t, copies):
        for cp in copies:
            cp.wait()
        for i, ref in enumerate((dk_ref, dv_ref)):
            s = acc_own[t, i]
            for p in range(1, chips):
                s = s + rs_in[t, p, i].astype(jnp.float32)
            acc_own[t, i] = s

    carry = remote(acc_own.at[0], acc_in.at[1], cs.at[0], cr.at[0], (prev, cx))
    sends = [[], []]
    for t in range(2):
        for cp in swaps[t]:
            cp.wait_recv()
        for a, b in split:
            for p in range(a, b):
                if t == 1 or p > 0:
                    for i in range(2):
                        gather[t][2 * (p - 1 + t) + i].wait_recv()
            for p in range(a, b):
                kt[:, pl.ds(p * ROWS, ROWS)] = kb[t, pl.ds(p * ROWS, ROWS), :].astype(jnp.float32).T.astype(
                    jnp.bfloat16
                )
            first_pass(t, a, b)
        stats(t)
        for n, (a, b) in enumerate(reversed(split)):
            second_pass(t, a, b, n == 0)
            sends[t] += send_terms(t, a, b)
        far = pl.ds(pl.multiple_of((1 - core) * HEADS * ROWS, HEADS * ROWS), HEADS * ROWS)
        dq_copy = remote(dqt.at[:, far], dq_in.at[t], dqs.at[t], dqr.at[t], partner)
        dq_copy.start()
        finish_queries(t, dq_copy)
        if t == 0:
            finish_terms(0, sends[0])
            acc_own[0] = acc_own[0] + acc_in[0]
            dk_ref[0, 0] = acc_own[0, 0]
            dv_ref[0, 0] = acc_own[0, 1]

            @pl.when(sec > 0)
            def _():
                carry.start()

    finish_terms(1, sends[1])

    @pl.when(sec < sections - 1)
    def _():
        carry.wait_recv()
        acc_own[1] = acc_own[1] + acc_in[1]

    dk_ref[1, 0] = acc_own[1, 0]
    dv_ref[1, 0] = acc_own[1, 1]

    @pl.when(sec > 0)
    def _():
        carry.wait_send()

    for t in range(2):
        for cp in gather[t] + swaps[t]:
            cp.wait_send()


def body(queries, out_grad, keys, values, entering_keys, entering_values, key_grads_in, value_grads_in, group_order, *, chips, sections):
    any_spec = pl.BlockSpec(memory_space=pl.ANY)
    vmem = pl.BlockSpec(memory_space=pltpu.VMEM)
    total = 2 * HEADS * ROWS
    bf16, f32 = jnp.bfloat16, jnp.float32
    dma = pltpu.SemaphoreType.DMA
    return pl.pallas_call(
        functools.partial(kernel, chips, sections),
        out_shape=(
            jax.ShapeDtypeStruct((2, 1, ROWS, HEADS * DIM), bf16),
            jax.ShapeDtypeStruct((2, 1, ROWS, DIM), f32),
            jax.ShapeDtypeStruct((2, 1, ROWS, DIM), f32),
        ),
        in_specs=[pl.BlockSpec(memory_space=pltpu.SMEM)] + [any_spec] * 8,
        out_specs=(vmem, vmem, vmem),
        scratch_shapes=[
            pltpu.VMEM((2, 2, HEADS, ROWS, DIM), bf16),
            pltpu.VMEM((2, 2, HEADS, ROWS, DIM), bf16),
            pltpu.VMEM((2, chips * ROWS, DIM), bf16),
            pltpu.VMEM((2, chips * ROWS, DIM), bf16),
            pltpu.VMEM((DIM, chips * ROWS), bf16),
            pltpu.VMEM((chips * ROWS, total), f32),
            pltpu.VMEM((chips * ROWS, total), f32),
            pltpu.VMEM((chips, total), f32),
            pltpu.VMEM((chips, total), f32),
            pltpu.VMEM((chips, total), f32),
            pltpu.VMEM((2, chips, total), f32),
            pltpu.VMEM((2, 8, total), f32),
            pltpu.VMEM((2, 8, total), f32),
            pltpu.VMEM((3 * ROWS, WIDE), bf16),
            pltpu.VMEM((3 * ROWS, WIDE), bf16),
            pltpu.VMEM((2, 3 * ROWS, DIM), f32),
            pltpu.VMEM((DIM, total), f32),
            pltpu.VMEM((2, DIM, total // 2), f32),
            pltpu.VMEM((2, chips, 2, ROWS, DIM), bf16),
            pltpu.VMEM((2, chips, 2, ROWS, DIM), bf16),
            pltpu.VMEM((2, 2, ROWS, DIM), f32),
            pltpu.VMEM((2, 2, ROWS, DIM), f32),
            dma((2, 2, HEADS)),
            dma((2,)),
            dma((2, 2, HEADS)),
            dma((2, 2, HEADS)),
            dma((2, chips, 2)),
            dma((2, chips, 2)),
            dma((2,)),
            dma((2,)),
            dma((2,)),
            dma((2,)),
            dma((2, chips)),
            dma((2, chips)),
            dma((1,)),
            dma((1,)),
            dma((2,)),
        ],
        compiler_params=pltpu.CompilerParams(
            collective_id=0, has_side_effects=True, vmem_limit_bytes=60 << 20
        ),
    )(group_order, queries, out_grad, keys, values, entering_keys, entering_values, key_grads_in, value_grads_in)


def solution(mesh):
    sections = mesh.shape["section"]
    chips = mesh.shape["ctx"] // 2
    return jax.shard_map(
        functools.partial(body, chips=chips, sections=sections),
        mesh=mesh,
        in_specs=(
            P(None, "section", "ctx", None),
            P(None, "section", "ctx", None),
            P("section", "ctx", None),
            P("section", "ctx", None),
            P("ctx", None),
            P("ctx", None),
            P("section", "ctx", None),
            P("section", "ctx", None),
            P(),
        ),
        out_specs=(
            P(None, "section", "ctx", None),
            P(None, "section", "ctx", None),
            P(None, "section", "ctx", None),
        ),
        check_vma=False,
    )
```

time: 222 us -> 82 us (0.37)
  waiting for transfers between devices: 118 us -> 0 us
  Pallas kernels: 0 us -> 77.7 us
  matrix products: 45.2 us -> 0 us
  starting transfers between devices: 24.8 us -> 0 us
  other arithmetic: 20 us -> 0 us
  local copies, waits for them, and re-layouts: 12.2 us -> 3.51 us
    all_to_all x4 -> x0, waiting for transfers between devices: 114 us -> none  [the longest x2 74.2 us: sum_at_owner(): parts = lax.all_to_all(split_up(array, dim, peers), axis, 0, 0, tiled=True)]
    pallas_call x0 -> x1, Pallas kernels: none -> 77.7 us  [body(): pl.pallas_call(functools.partial(kernel, chips, sections), out_shape=(jax...]
    dot_general x10 -> x0, matrix products: 45.2 us -> none  [the longest x2 12.2 us: one_tick(): jnp.dot(grads_flat, value_block.T, preferred_element_type=jnp.float32)]
    all_to_all x4 -> x0, starting transfers between devices: 22.2 us -> none  [the longest x2 13.5 us: copy_for_each(): return lax.all_to_all(copies, axis, split_axis=0, concat_axis=0, tiled=True)]
    convert_element_type x1 -> x0, other arithmetic: 11.2 us -> none  [one_tick(): score_grad = (probs * (prob_grads - deltas)).astype(jnp.bfloat16)]
    ppermute x2 -> x0, waiting for transfers between devices: 4.13 us -> none  [shifted(): return lax.ppermute(block, axis, route)]
    another operation x8 -> x0, local copies, waits for them, and re-layouts: 4.01 us -> none  [the longest x2 2.13 us: body(): query_grads = jnp.stack([first_query, second_query], axis=0)[:, None]]
    reduce_sum x4 -> x0, other arithmetic: 3.2 us -> none  [the longest x2 1.81 us: sum_at_owner(): return jnp.sum(parts, axis=0)]
  transfers between devices with their start and end apart: 6 -> 0, of which waited for: 5 -> 0; matrix products, arithmetic and copies ran while one was open for 15% -> 0% of each run, Pallas kernels for 0% -> 0%
where the time goes in v1:
time: 82 us; the launch traced here: 81.9 us
  Pallas kernels  77.7 us (95%)
  local copies, waits for them, and re-layouts  3.51 us (4%)
    pallas_call x1, Pallas kernels, body(): pl.pallas_call(functools.partial(kernel, chips, sections), out_shape=(jax...  77.7 us
    unnamed x7, local copies, waits for them, and re-layouts  3.51 us

profile of v1, /device:TPU:1, one launch (start us, length us, event | category | flops | bytes accessed | tf_op | source)
XLA Modules:
  0.0 81.9 jit_solution(11085580154444449799)
XLA Ops:
  0.6 77.7 %shard_map.112 = (bf16[2,1,128,1024]{3,2,1,0:T(8,128)(2,1)}, f32[2,1,128,128]{3,2,1,0:T(8,128)}, f32[2,1,128,128]{3,2,1,0:T(8,128)}) custom-call(s32[16]{0:T(128)} %order_ref.1, bf16[2,1,128,1024]{3,2,1,0:T(8,128)(2,1)} %q_ref.1, bf16[2,1,128,1024]{3,2,1,0:T(8,128)(2,1)} %g_ref.1, bf16[1,128,128]{2,1,0:T(8,128)(2,1)} %k_ref.1, bf16[1,128,128]{2,1,0:T(8,128)(2,1)} %v_ref.1, ...), custom_call_target="tpu_custom_call" | custom-call | tf_op jit(solution)/shard_map/pallas_call | solution.py:363
  78.4 0.0 copy-start.1
  78.4 1.9 %copy.15 = bf16[2,1,128,1024]{3,2,1,0:T(8,128)(2,1)} copy(bf16[2,1,128,1024]{3,2,1,0:T(8,128)(2,1)} %get-tuple-element.6) | data formatting | bytes 1048576
  80.3 0.0 copy-done.1
  80.3 0.0 copy-start
  80.3 0.7 copy.16
  81.0 0.3 copy-done
  81.3 0.7 copy.17
Async XLA Ops:
  78.4 1.9 %copy-start.1 = (f32[2,1,128,128]{3,2,1,0:T(8,128)S(1)}, f32[2,1,128,128]{3,2,1,0:T(8,128)}, u32[]{:S(2)}) copy-start(f32[2,1,128,128]{3,2,1,0:T(8,128)} %get-tuple-element.7) | copy-start | bytes 393220
  80.3 1.0 %copy-start = (f32[2,1,128,128]{3,2,1,0:T(8,128)S(1)}, f32[2,1,128,128]{3,2,1,0:T(8,128)}, u32[]{:S(2)}) copy-start(f32[2,1,128,128]{3,2,1,0:T(8,128)} %get-tuple-element.8) | copy-start | bytes 393220

commit v2 on v1

--- a/solution.py
+++ b/solution.py
@@ -25,15 +25,12 @@
     return lax.dot_general(a, b, dims, preferred_element_type=jnp.float32)
 
 
-def offsets_of(chips):
-    out = [0]
-    for d in range(1, chips // 2):
-        out += [d, -d]
-    return out + [chips // 2]
+OFFSETS = (0, 1, -1, 2, -2, 3, -3, 4)
+CHIPS = len(OFFSETS)
+NEAR = (3, 4, 1, 2)
 
 
 def kernel(
-    chips,
     sections,
     order_ref,
     q_ref,
@@ -67,6 +64,9 @@
     dq_in,
     rs_out,
     rs_in,
+    rs_mid,
+    rs_far,
+    mid_own,
     acc_own,
     acc_in,
     load_sem,
@@ -85,8 +85,6 @@
     cr,
     acc_sem,
 ):
-    offsets = offsets_of(chips)
-    split = [(0, 3), (3, 5), (5, 8)] if chips == 8 else [(0, 3), (3, 4)]
     sec = lax.axis_index("section")
     cx = lax.axis_index("ctx")
     chip = cx // 2
@@ -96,15 +94,15 @@
     partner = (sec, chip * 2 + 1 - core)
 
     def peer(section, offset):
-        return (section, lax.rem(chip + offset + chips, chips) * 2 + core)
+        return (section, lax.rem(chip + offset + CHIPS, CHIPS) * 2 + core)
 
     barrier = pltpu.get_barrier_semaphore()
-    for off in offsets[1:]:
-        pl.semaphore_signal(barrier, inc=1, device_id=peer(sec, off), device_id_type=MESH)
+    for p in range(1, 5):
+        pl.semaphore_signal(barrier, inc=1, device_id=peer(sec, OFFSETS[p]), device_id_type=MESH)
     pl.semaphore_signal(barrier, inc=1, device_id=partner, device_id_type=MESH)
-    for off in offsets:
-        pl.semaphore_signal(barrier, inc=1, device_id=peer(nxt, off), device_id_type=MESH)
-        pl.semaphore_signal(barrier, inc=1, device_id=peer(prev, off), device_id_type=MESH)
+    for p in range(5):
+        pl.semaphore_signal(barrier, inc=1, device_id=peer(nxt, OFFSETS[p]), device_id_type=MESH)
+        pl.semaphore_signal(barrier, inc=1, device_id=peer(prev, OFFSETS[p]), device_id_type=MESH)
 
     def local(src, dst, sem):
         return pltpu.make_async_copy(src, dst, sem)
@@ -136,16 +134,20 @@
     for cp in own_kv + loads + acc_loads:
         cp.start()
 
-    pl.semaphore_wait(barrier, (chips - 1) + 1 + 2 * chips)
-
-    gather = [[], []]
-    for p in range(1, chips):
-        dev = peer(sec, offsets[p])
+    pl.semaphore_wait(barrier, 15)
+
+    def kv_copies(t, p, dev, k_src, v_src):
         rows = pl.ds(p * ROWS, ROWS)
-        gather[0].append(remote(k_ref.at[0], kb.at[0, rows], ags.at[0, p, 0], agr.at[0, p, 0], dev))
-        gather[0].append(remote(v_ref.at[0], vb.at[0, rows], ags.at[0, p, 1], agr.at[0, p, 1], dev))
-    for cp in gather[0]:
-        cp.start()
+        return [
+            remote(k_src, kb.at[t, rows], ags.at[t, p, 0], agr.at[t, p, 0], dev),
+            remote(v_src, vb.at[t, rows], ags.at[t, p, 1], agr.at[t, p, 1], dev),
+        ]
+
+    gather = [{}, {}]
+    for p in NEAR:
+        gather[0][p] = kv_copies(0, p, peer(sec, OFFSETS[p]), k_ref.at[0], v_ref.at[0])
+        for cp in gather[0][p]:
+            cp.start()
 
     swaps = [[], []]
     for t in range(2):
@@ -164,25 +166,42 @@
         cp.start()
 
     def next_gather(k_src, v_src):
-        out = []
-        for p in range(chips):
-            dev = peer(prev, offsets[p])
+        return {p: kv_copies(1, p, peer(prev, OFFSETS[p]), k_src, v_src) for p in NEAR + (0,)}
+
+    def start_next_gather():
+        @pl.when(sec > 0)
+        def _():
+            for cps in next_gather(k_ref.at[0], v_ref.at[0]).values():
+                for cp in cps:
+                    cp.start()
+
+        @pl.when(sec == 0)
+        def _():
+            for cps in next_gather(ek_ref, ev_ref).values():
+                for cp in cps:
+                    cp.start()
+
+        gather[1].update(next_gather(k_ref.at[0], v_ref.at[0]))
+
+    def relay_gather(t):
+        for p, near, far in ((3, 1, 5), (4, 2, 6)):
+            for cp in gather[t][p]:
+                cp.wait_recv()
             rows = pl.ds(p * ROWS, ROWS)
-            out.append(remote(k_src, kb.at[1, rows], ags.at[1, p, 0], agr.at[1, p, 0], dev))
-            out.append(remote(v_src, vb.at[1, rows], ags.at[1, p, 1], agr.at[1, p, 1], dev))
-        return out
-
-    @pl.when(sec > 0)
-    def _():
-        for cp in next_gather(k_ref.at[0], v_ref.at[0]):
+            k_src, v_src = kb.at[t, rows], vb.at[t, rows]
+            gather[t][far] = kv_copies(t, far, peer(sec, OFFSETS[near]), k_src, v_src)
+            for cp in gather[t][far]:
+                cp.start()
+            half = p - 3
+            cp = kv_copies(t, 7, peer(sec, OFFSETS[p]), k_src, v_src)[half]
             cp.start()
-
-    @pl.when(sec == 0)
-    def _():
-        for cp in next_gather(ek_ref, ev_ref):
-            cp.start()
-
-    gather[1] = next_gather(k_ref.at[0], v_ref.at[0])
+            gather[t].setdefault(7, []).append(cp)
+
+    def wait_keys(t, ps):
+        for p in ps:
+            for cp in gather[t].get(p, []):
+                cp.wait_recv()
+
     for cp in swaps[1]:
         cp.start()
     for cp in own_kv + loads + acc_loads:
@@ -195,7 +214,7 @@
     total = 2 * HEADS * ROWS
 
     def key_group(p):
-        return order_ref[lax.rem(chip - offsets[p] + chips, chips) * 2 + core]
+        return order_ref[lax.rem(chip - OFFSETS[p] + CHIPS, CHIPS) * 2 + core]
 
     def first_pass(t, a, b):
         keys = kb[t, pl.ds(a * ROWS, (b - a) * ROWS), :]
@@ -242,7 +261,7 @@
         inv = 1.0 / (l_own * w_own + st_in[t, 1:2, :] * w_far)
         delta = (d_own * w_own + st_in[t, 2:3, :] * w_far) * inv
         fst[0] = jnp.exp2((m_b - m) * c_exp) * inv
-        fst[1] = jnp.broadcast_to(delta, (chips, total))
+        fst[1] = jnp.broadcast_to(delta, (CHIPS, total))
 
     def second_pass(t, a, b, first):
         m_rows = (b - a) * ROWS
@@ -265,77 +284,130 @@
             acc[1, pl.ds(0, m_rows), :] += mm(pr, gb[t, half, group].reshape(WIDE, DIM))
             part = mm(kt[:, pl.ds(a * ROWS, m_rows)], sg)
             if first:
-                dqt[:, lanes] = part
+                dqt[t, :, lanes] = part
             else:
-                dqt[:, lanes] += part
+                dqt[t, :, lanes] += part
+
+    sends = [[], []]
+    middle = [[], []]
+
+    def push(t, src, buf, slot, sem_slot, dev, keep):
+        cp = remote(src, buf.at[slot], rss.at[t, sem_slot], rsr.at[t, sem_slot], dev)
+        cp.start()
+        keep.append(cp)
 
     def send_terms(t, a, b):
-        out = []
         for p in range(a, b):
             rows = pl.ds((p - a) * ROWS, ROWS)
+            dk = acc[0, rows, :] * SCALE
+            dv = acc[1, rows, :]
             if p == 0:
-                acc_own[t, 0] = acc[0, rows, :] * SCALE
-                acc_own[t, 1] = acc[1, rows, :]
+                acc_own[t, 0] = dk
+                acc_own[t, 1] = dv
+            elif p in (3, 4):
+                mid_own[p - 3, 0] = dk
+                mid_own[p - 3, 1] = dv
             else:
-                rs_out[t, p, 0] = (acc[0, rows, :] * SCALE).astype(jnp.bfloat16)
-                rs_out[t, p, 1] = acc[1, rows, :].astype(jnp.bfloat16)
-                cp = remote(
-                    rs_out.at[t, p], rs_in.at[t, p], rss.at[t, p], rsr.at[t, p], peer(sec, -offsets[p])
-                )
-                cp.start()
-                out.append(cp)
-        return out
-
-    def finish_queries(t, cp):
-        cp.wait()
+                rs_out[t, p, 0] = dk.astype(jnp.bfloat16)
+                rs_out[t, p, 1] = dv.astype(jnp.bfloat16)
+                if p < 3:
+                    push(t, rs_out.at[t, p], rs_in, (t, p), p, peer(sec, -OFFSETS[p]), sends[t])
+                elif p < 7:
+                    near = p - 4
+                    push(t, rs_out.at[t, p], rs_mid, (t, p - 5), p, peer(sec, -OFFSETS[near]), middle[t])
+                else:
+                    push(t, rs_out.at[t, p, 0], rs_far, (t, 0), 7, peer(sec, -2), middle[t])
+                    push(t, rs_out.at[t, p, 1], rs_far, (t, 1), 0, peer(sec, 2), middle[t])
+
+    def relay_terms(t):
+        for cp in middle[t]:
+            cp.wait_recv()
+        for p in (3, 4):
+            n = p - 3
+            dk = mid_own[n, 0] + rs_mid[t, n, 0].astype(jnp.float32)
+            dv = mid_own[n, 1] + rs_mid[t, n, 1].astype(jnp.float32)
+            far = rs_far[t, n].astype(jnp.float32)
+            if n == 0:
+                dk = dk + far
+            else:
+                dv = dv + far
+            rs_out[t, p, 0] = dk.astype(jnp.bfloat16)
+            rs_out[t, p, 1] = dv.astype(jnp.bfloat16)
+            push(t, rs_out.at[t, p], rs_in, (t, p), p, peer(sec, -OFFSETS[p]), sends[t])
+
+    far_rows = pl.ds(pl.multiple_of((1 - core) * HEADS * ROWS, HEADS * ROWS), HEADS * ROWS)
+    dq_copies = [
+        remote(dqt.at[t, :, far_rows], dq_in.at[t], dqs.at[t], dqr.at[t], partner) for t in range(2)
+    ]
+
+    def finish_queries(t):
+        dq_copies[t].wait()
         for h in range(HEADS):
             own = pl.ds(pl.multiple_of(core * HEADS * ROWS + h * ROWS, ROWS), ROWS)
-            full = (dqt[:, own] + dq_in[t, :, pl.ds(h * ROWS, ROWS)]) * SCALE
+            full = (dqt[t, :, own] + dq_in[t, :, pl.ds(h * ROWS, ROWS)]) * SCALE
             dq_ref[t, 0, :, pl.ds(h * DIM, DIM)] = full.T.astype(jnp.bfloat16)
 
-    def finish_terms(t, copies):
-        for cp in copies:
-            cp.wait()
-        for i, ref in enumerate((dk_ref, dv_ref)):
+    def finish_terms(t):
+        for cp in sends[t]:
+            cp.wait_recv()
+        for i in range(2):
             s = acc_own[t, i]
-            for p in range(1, chips):
+            for p in range(1, 5):
                 s = s + rs_in[t, p, i].astype(jnp.float32)
+            if t == 0:
+                s = s + acc_in[0, i]
             acc_own[t, i] = s
 
     carry = remote(acc_own.at[0], acc_in.at[1], cs.at[0], cr.at[0], (prev, cx))
-    sends = [[], []]
-    for t in range(2):
+    def make_transposed(t):
+        for p in range(CHIPS):
+            rows = pl.ds(p * ROWS, ROWS)
+            kt[:, rows] = kb[t, rows, :].astype(jnp.float32).T.astype(jnp.bfloat16)
+
+    def swap_wait(t):
         for cp in swaps[t]:
             cp.wait_recv()
-        for a, b in split:
-            for p in range(a, b):
-                if t == 1 or p > 0:
-                    for i in range(2):
-                        gather[t][2 * (p - 1 + t) + i].wait_recv()
-            for p in range(a, b):
-                kt[:, pl.ds(p * ROWS, ROWS)] = kb[t, pl.ds(p * ROWS, ROWS), :].astype(jnp.float32).T.astype(
-                    jnp.bfloat16
-                )
-            first_pass(t, a, b)
-        stats(t)
-        for n, (a, b) in enumerate(reversed(split)):
+
+    def all_second(t):
+        for n, (a, b) in enumerate(((5, 8), (0, 3), (3, 5))):
             second_pass(t, a, b, n == 0)
-            sends[t] += send_terms(t, a, b)
-        far = pl.ds(pl.multiple_of((1 - core) * HEADS * ROWS, HEADS * ROWS), HEADS * ROWS)
-        dq_copy = remote(dqt.at[:, far], dq_in.at[t], dqs.at[t], dqr.at[t], partner)
-        dq_copy.start()
-        finish_queries(t, dq_copy)
-        if t == 0:
-            finish_terms(0, sends[0])
-            acc_own[0] = acc_own[0] + acc_in[0]
-            dk_ref[0, 0] = acc_own[0, 0]
-            dv_ref[0, 0] = acc_own[0, 1]
-
-            @pl.when(sec > 0)
-            def _():
-                carry.start()
-
-    finish_terms(1, sends[1])
+            send_terms(t, a, b)
+        dq_copies[t].start()
+
+    swap_wait(0)
+    first_pass(0, 0, 1)
+    relay_gather(0)
+    start_next_gather()
+    wait_keys(0, (1, 2))
+    first_pass(0, 1, 5)
+    wait_keys(0, (5, 6, 7))
+    first_pass(0, 5, 8)
+    make_transposed(0)
+    stats(0)
+    all_second(0)
+
+    relay_gather(1)
+    swap_wait(1)
+    wait_keys(1, (0, 1, 2))
+    first_pass(1, 0, 5)
+    relay_terms(0)
+    wait_keys(1, (5, 6, 7))
+    first_pass(1, 5, 8)
+    make_transposed(1)
+    finish_queries(0)
+    finish_terms(0)
+    dk_ref[0, 0] = acc_own[0, 0]
+    dv_ref[0, 0] = acc_own[0, 1]
+
+    @pl.when(sec > 0)
+    def _():
+        carry.start()
+
+    stats(1)
+    all_second(1)
+    relay_terms(1)
+    finish_queries(1)
+    finish_terms(1)
 
     @pl.when(sec < sections - 1)
     def _():
@@ -350,18 +422,21 @@
         carry.wait_send()
 
     for t in range(2):
-        for cp in gather[t] + swaps[t]:
+        for cps in gather[t].values():
+            for cp in cps:
+                cp.wait_send()
+        for cp in swaps[t] + middle[t] + sends[t]:
             cp.wait_send()
 
 
-def body(queries, out_grad, keys, values, entering_keys, entering_values, key_grads_in, value_grads_in, group_order, *, chips, sections):
+def body(queries, out_grad, keys, values, entering_keys, entering_values, key_grads_in, value_grads_in, group_order, *, sections):
     any_spec = pl.BlockSpec(memory_space=pl.ANY)
     vmem = pl.BlockSpec(memory_space=pltpu.VMEM)
     total = 2 * HEADS * ROWS
     bf16, f32 = jnp.bfloat16, jnp.float32
     dma = pltpu.SemaphoreType.DMA
     return pl.pallas_call(
-        functools.partial(kernel, chips, sections),
+        functools.partial(kernel, sections),
         out_shape=(
             jax.ShapeDtypeStruct((2, 1, ROWS, HEADS * DIM), bf16),
             jax.ShapeDtypeStruct((2, 1, ROWS, DIM), f32),
@@ -372,38 +447,41 @@
         scratch_shapes=[
             pltpu.VMEM((2, 2, HEADS, ROWS, DIM), bf16),
             pltpu.VMEM((2, 2, HEADS, ROWS, DIM), bf16),
-            pltpu.VMEM((2, chips * ROWS, DIM), bf16),
-            pltpu.VMEM((2, chips * ROWS, DIM), bf16),
-            pltpu.VMEM((DIM, chips * ROWS), bf16),
-            pltpu.VMEM((chips * ROWS, total), f32),
-            pltpu.VMEM((chips * ROWS, total), f32),
-            pltpu.VMEM((chips, total), f32),
-            pltpu.VMEM((chips, total), f32),
-            pltpu.VMEM((chips, total), f32),
-            pltpu.VMEM((2, chips, total), f32),
+            pltpu.VMEM((2, CHIPS * ROWS, DIM), bf16),
+            pltpu.VMEM((2, CHIPS * ROWS, DIM), bf16),
+            pltpu.VMEM((DIM, CHIPS * ROWS), bf16),
+            pltpu.VMEM((CHIPS * ROWS, total), f32),
+            pltpu.VMEM((CHIPS * ROWS, total), f32),
+            pltpu.VMEM((CHIPS, total), f32),
+            pltpu.VMEM((CHIPS, total), f32),
+            pltpu.VMEM((CHIPS, total), f32),
+            pltpu.VMEM((2, CHIPS, total), f32),
             pltpu.VMEM((2, 8, total), f32),
             pltpu.VMEM((2, 8, total), f32),
             pltpu.VMEM((3 * ROWS, WIDE), bf16),
             pltpu.VMEM((3 * ROWS, WIDE), bf16),
             pltpu.VMEM((2, 3 * ROWS, DIM), f32),
-            pltpu.VMEM((DIM, total), f32),
+            pltpu.VMEM((2, DIM, total), f32),
             pltpu.VMEM((2, DIM, total // 2), f32),
-            pltpu.VMEM((2, chips, 2, ROWS, DIM), bf16),
-            pltpu.VMEM((2, chips, 2, ROWS, DIM), bf16),
+            pltpu.VMEM((2, CHIPS, 2, ROWS, DIM), bf16),
+            pltpu.VMEM((2, 5, 2, ROWS, DIM), bf16),
+            pltpu.VMEM((2, 2, 2, ROWS, DIM), bf16),
+            pltpu.VMEM((2, 2, ROWS, DIM), bf16),
+            pltpu.VMEM((2, 2, ROWS, DIM), f32),
             pltpu.VMEM((2, 2, ROWS, DIM), f32),
             pltpu.VMEM((2, 2, ROWS, DIM), f32),
             dma((2, 2, HEADS)),
             dma((2,)),
             dma((2, 2, HEADS)),
             dma((2, 2, HEADS)),
-            dma((2, chips, 2)),
-            dma((2, chips, 2)),
+            dma((2, CHIPS, 2)),
+            dma((2, CHIPS, 2)),
             dma((2,)),
             dma((2,)),
             dma((2,)),
             dma((2,)),
-            dma((2, chips)),
-            dma((2, chips)),
+            dma((2, CHIPS)),
+            dma((2, CHIPS)),
             dma((1,)),
             dma((1,)),
             dma((2,)),
@@ -416,9 +494,8 @@
 
 def solution(mesh):
     sections = mesh.shape["section"]
-    chips = mesh.shape["ctx"] // 2
     return jax.shard_map(
-        functools.partial(body, chips=chips, sections=sections),
+        functools.partial(body, sections=sections),
         mesh=mesh,
         in_specs=(
             P(None, "section", "ctx", None),

time: 82 us -> 63.4 us (0.77)
  Pallas kernels: 77.7 us -> 59.1 us
    pallas_call x1, Pallas kernels: 77.7 us -> 59.1 us  [body(): pl.pallas_call(functools.partial(kernel, sections), out_shape=(jax.ShapeD...]
where the time goes in v2:
time: 63.4 us; the launch traced here: 63.3 us
  Pallas kernels  59.1 us (93%)
  local copies, waits for them, and re-layouts  3.51 us (6%)
  between operations  0.65 us (1%)
    pallas_call x1, Pallas kernels, body(): pl.pallas_call(functools.partial(kernel, sections), out_shape=(jax.ShapeD...  59.1 us
    unnamed x7, local copies, waits for them, and re-layouts  3.51 us

profile of v2, /device:TPU:1, one launch (start us, length us, event | category | flops | bytes accessed | tf_op | source)
XLA Modules:
  0.0 63.3 jit_solution(9533998684617609197)
XLA Ops:
  0.6 59.1 %shard_map.112 = (bf16[2,1,128,1024]{3,2,1,0:T(8,128)(2,1)}, f32[2,1,128,128]{3,2,1,0:T(8,128)}, f32[2,1,128,128]{3,2,1,0:T(8,128)}) custom-call(s32[16]{0:T(128)} %order_ref.1, bf16[2,1,128,1024]{3,2,1,0:T(8,128)(2,1)} %q_ref.1, bf16[2,1,128,1024]{3,2,1,0:T(8,128)(2,1)} %g_ref.1, bf16[1,128,128]{2,1,0:T(8,128)(2,1)} %k_ref.1, bf16[1,128,128]{2,1,0:T(8,128)(2,1)} %v_ref.1, ...), custom_call_target="tpu_custom_call" | custom-call | tf_op jit(solution)/shard_map/pallas_call | solution.py:438
  59.8 0.0 copy-start.1
  59.8 1.9 %copy.15 = bf16[2,1,128,1024]{3,2,1,0:T(8,128)(2,1)} copy(bf16[2,1,128,1024]{3,2,1,0:T(8,128)(2,1)} %get-tuple-element.6) | data formatting | bytes 1048576
  61.7 0.0 copy-done.1
  61.7 0.0 copy-start
  61.7 0.7 %copy.16 = f32[2,1,128,128]{3,2,1,0:T(8,128)} copy(f32[2,1,128,128]{3,2,1,0:T(8,128)S(1)} %copy-done.1) | data formatting | bytes 262144
  62.3 0.3 copy-done
  62.6 0.7 %copy.17 = f32[2,1,128,128]{3,2,1,0:T(8,128)} copy(f32[2,1,128,128]{3,2,1,0:T(8,128)S(1)} %copy-done) | data formatting | bytes 262144
Async XLA Ops:
  59.8 1.9 %copy-start.1 = (f32[2,1,128,128]{3,2,1,0:T(8,128)S(1)}, f32[2,1,128,128]{3,2,1,0:T(8,128)}, u32[]{:S(2)}) copy-start(f32[2,1,128,128]{3,2,1,0:T(8,128)} %get-tuple-element.7) | copy-start | bytes 393220
  61.7 1.0 %copy-start = (f32[2,1,128,128]{3,2,1,0:T(8,128)S(1)}, f32[2,1,128,128]{3,2,1,0:T(8,128)}, u32[]{:S(2)}) copy-start(f32[2,1,128,128]{3,2,1,0:T(8,128)} %get-tuple-element.8) | copy-start | bytes 393220

commit v3 on v2

--- a/solution.py
+++ b/solution.py
@@ -13,6 +13,8 @@
 ROWS = 128
 CHUNK = 256
 WIDE = 512
+UNROLL = 2
+UNROLL2 = 2
 NEG = -1e30
 MESH = pl.DeviceIdType.MESH
 SCALE = 1.0 / math.sqrt(DIM)
@@ -100,9 +102,8 @@
     for p in range(1, 5):
         pl.semaphore_signal(barrier, inc=1, device_id=peer(sec, OFFSETS[p]), device_id_type=MESH)
     pl.semaphore_signal(barrier, inc=1, device_id=partner, device_id_type=MESH)
-    for p in range(5):
-        pl.semaphore_signal(barrier, inc=1, device_id=peer(nxt, OFFSETS[p]), device_id_type=MESH)
-        pl.semaphore_signal(barrier, inc=1, device_id=peer(prev, OFFSETS[p]), device_id_type=MESH)
+    pl.semaphore_signal(barrier, inc=1, device_id=(nxt, cx), device_id_type=MESH)
+    pl.semaphore_signal(barrier, inc=1, device_id=(prev, cx), device_id_type=MESH)
 
     def local(src, dst, sem):
         return pltpu.make_async_copy(src, dst, sem)
@@ -134,7 +135,7 @@
     for cp in own_kv + loads + acc_loads:
         cp.start()
 
-    pl.semaphore_wait(barrier, 15)
+    pl.semaphore_wait(barrier, 7)
 
     def kv_copies(t, p, dev, k_src, v_src):
         rows = pl.ds(p * ROWS, ROWS)
@@ -165,23 +166,29 @@
     for cp in swaps[0]:
         cp.start()
 
-    def next_gather(k_src, v_src):
-        return {p: kv_copies(1, p, peer(prev, OFFSETS[p]), k_src, v_src) for p in NEAR + (0,)}
+    def shift_keys(k_src, v_src):
+        return kv_copies(1, 0, (prev, cx), k_src, v_src)
+
+    @pl.when(sec > 0)
+    def _():
+        for cp in shift_keys(k_ref.at[0], v_ref.at[0]):
+            cp.start()
+
+    @pl.when(sec == 0)
+    def _():
+        for cp in shift_keys(ek_ref, ev_ref):
+            cp.start()
+
+    gather[1][0] = shift_keys(k_ref.at[0], v_ref.at[0])
 
     def start_next_gather():
-        @pl.when(sec > 0)
-        def _():
-            for cps in next_gather(k_ref.at[0], v_ref.at[0]).values():
-                for cp in cps:
-                    cp.start()
-
-        @pl.when(sec == 0)
-        def _():
-            for cps in next_gather(ek_ref, ev_ref).values():
-                for cp in cps:
-                    cp.start()
-
-        gather[1].update(next_gather(k_ref.at[0], v_ref.at[0]))
+        for cp in gather[1][0]:
+            cp.wait_recv()
+        rows = pl.ds(0, ROWS)
+        for p in NEAR:
+            gather[1][p] = kv_copies(1, p, peer(sec, OFFSETS[p]), kb.at[1, rows], vb.at[1, rows])
+            for cp in gather[1][p]:
+                cp.start()
 
     def relay_gather(t):
         for p, near, far in ((3, 1, 5), (4, 2, 6)):
@@ -220,7 +227,7 @@
         keys = kb[t, pl.ds(a * ROWS, (b - a) * ROWS), :]
         values = vb[t, pl.ds(a * ROWS, (b - a) * ROWS), :]
 
-        @pl.loop(0, total // CHUNK)
+        @pl.loop(0, total // CHUNK, unroll=UNROLL)
         def _(j):
             half = j // (HEADS // 2)
             pair = pl.ds(lax.rem(j, HEADS // 2) * 2, 2)
@@ -232,27 +239,32 @@
             query_group = order_ref[chip * 2 + half]
             for p in range(a, b):
                 part = slice((p - a) * ROWS, (p - a + 1) * ROWS)
-                limit = (query_group - key_group(p)) * ROWS
-                s = jnp.where(diff <= limit, s_all[part], NEG)
+                ahead = query_group - key_group(p)
+                s = s_all[part]
+                if p == 0:
+                    s = jnp.where(diff <= ahead * ROWS, s, NEG)
                 m = jnp.max(s, axis=0, keepdims=True)
                 e = jnp.exp2((s - m) * c_exp)
                 d = d_all[part]
-                eb[pl.ds(p * ROWS, ROWS), lanes] = e
-                db[pl.ds(p * ROWS, ROWS), lanes] = d
-                mst[pl.ds(p, 1), lanes] = m
-                lst[pl.ds(p, 1), lanes] = jnp.sum(e, axis=0, keepdims=True)
-                dsum[pl.ds(p, 1), lanes] = jnp.sum(e * d, axis=0, keepdims=True)
-
-    def stats(t):
-        m_b = mst[...]
+                eb[t, pl.ds(p * ROWS, ROWS), lanes] = e
+                db[t, pl.ds(p * ROWS, ROWS), lanes] = d
+                if p > 0:
+                    m = jnp.where(ahead > 0, m, NEG)
+                mst[t, pl.ds(p, 1), lanes] = m
+                lst[t, pl.ds(p, 1), lanes] = jnp.sum(e, axis=0, keepdims=True)
+                dsum[t, pl.ds(p, 1), lanes] = jnp.sum(e * d, axis=0, keepdims=True)
+
+    def stats(t, meanwhile):
+        m_b = mst[t]
         m_own = jnp.max(m_b, axis=0, keepdims=True)
         w = jnp.exp2((m_b - m_own) * c_exp)
-        l_own = jnp.sum(lst[...] * w, axis=0, keepdims=True)
-        d_own = jnp.sum(dsum[...] * w, axis=0, keepdims=True)
+        l_own = jnp.sum(lst[t] * w, axis=0, keepdims=True)
+        d_own = jnp.sum(dsum[t] * w, axis=0, keepdims=True)
         row = lax.broadcasted_iota(jnp.int32, (8, total), 0)
         st_out[t] = jnp.where(row == 0, m_own, jnp.where(row == 1, l_own, d_own))
         cp = remote(st_out.at[t], st_in.at[t], sts.at[t], stv.at[t], partner)
         cp.start()
+        meanwhile()
         cp.wait()
         m_far = st_in[t, 0:1, :]
         m = jnp.maximum(m_own, m_far)
@@ -263,30 +275,33 @@
         fst[0] = jnp.exp2((m_b - m) * c_exp) * inv
         fst[1] = jnp.broadcast_to(delta, (CHIPS, total))
 
-    def second_pass(t, a, b, first):
+    def second_pass(t, a, b):
         m_rows = (b - a) * ROWS
         acc[...] = jnp.zeros_like(acc)
 
-        @pl.loop(0, total // WIDE)
+        @pl.loop(0, total // WIDE, unroll=UNROLL2)
         def _(j):
             lanes = pl.ds(pl.multiple_of(j * WIDE, WIDE), WIDE)
             half = j // (HEADS // 4)
             group = pl.ds(lax.rem(j, HEADS // 4) * 4, 4)
             delta = fst[1, 0:1, lanes]
             for p in range(a, b):
-                prob = eb[pl.ds(p * ROWS, ROWS), lanes] * fst[0, p : p + 1, lanes]
-                ds = prob * (db[pl.ds(p * ROWS, ROWS), lanes] - delta)
+                prob = eb[t, pl.ds(p * ROWS, ROWS), lanes] * fst[0, p : p + 1, lanes]
+                ds = prob * (db[t, pl.ds(p * ROWS, ROWS), lanes] - delta)
                 pbuf[pl.ds((p - a) * ROWS, ROWS), :] = prob.astype(jnp.bfloat16)
-                sbuf[pl.ds((p - a) * ROWS, ROWS), :] = ds.astype(jnp.bfloat16)
+                sbuf[pl.ds(p * ROWS, ROWS), lanes] = ds.astype(jnp.bfloat16)
             pr = pbuf[pl.ds(0, m_rows), :]
-            sg = sbuf[pl.ds(0, m_rows), :]
+            sg = sbuf[pl.ds(a * ROWS, m_rows), lanes]
             acc[0, pl.ds(0, m_rows), :] += mm(sg, qb[t, half, group].reshape(WIDE, DIM))
             acc[1, pl.ds(0, m_rows), :] += mm(pr, gb[t, half, group].reshape(WIDE, DIM))
-            part = mm(kt[:, pl.ds(a * ROWS, m_rows)], sg)
-            if first:
-                dqt[t, :, lanes] = part
-            else:
-                dqt[t, :, lanes] += part
+
+    def query_terms(t):
+        @pl.loop(0, total // WIDE, unroll=UNROLL2)
+        def _(j):
+            lanes = pl.ds(pl.multiple_of(j * WIDE, WIDE), WIDE)
+            dqt[t, :, lanes] = mm(kt[t], sbuf[:, lanes])
+
+        dq_copies[t].start()
 
     sends = [[], []]
     middle = [[], []]
@@ -359,42 +374,50 @@
             acc_own[t, i] = s
 
     carry = remote(acc_own.at[0], acc_in.at[1], cs.at[0], cr.at[0], (prev, cx))
-    def make_transposed(t):
-        for p in range(CHIPS):
+    def make_transposed(t, ps):
+        for p in ps:
             rows = pl.ds(p * ROWS, ROWS)
-            kt[:, rows] = kb[t, rows, :].astype(jnp.float32).T.astype(jnp.bfloat16)
+            kt[t, :, rows] = kb[t, rows, :].astype(jnp.float32).T.astype(jnp.bfloat16)
 
     def swap_wait(t):
         for cp in swaps[t]:
             cp.wait_recv()
 
     def all_second(t):
-        for n, (a, b) in enumerate(((5, 8), (0, 3), (3, 5))):
-            second_pass(t, a, b, n == 0)
+        for a, b in ((5, 8), (0, 3), (3, 5)):
+            second_pass(t, a, b)
             send_terms(t, a, b)
-        dq_copies[t].start()
+
+    def ahead():
+        make_transposed(0, (5, 6, 7))
+        relay_gather(1)
+        wait_keys(1, (1, 2))
+        first_pass(1, 1, 5)
+
+    def between():
+        relay_terms(0)
+        query_terms(0)
+        make_transposed(1, range(1, CHIPS))
 
     swap_wait(0)
     first_pass(0, 0, 1)
+    make_transposed(0, (0,))
     relay_gather(0)
     start_next_gather()
+    swap_wait(1)
+    first_pass(1, 0, 1)
+    make_transposed(1, (0,))
     wait_keys(0, (1, 2))
     first_pass(0, 1, 5)
+    make_transposed(0, (1, 2, 3, 4))
     wait_keys(0, (5, 6, 7))
     first_pass(0, 5, 8)
-    make_transposed(0)
-    stats(0)
+    stats(0, ahead)
     all_second(0)
-
-    relay_gather(1)
-    swap_wait(1)
-    wait_keys(1, (0, 1, 2))
-    first_pass(1, 0, 5)
-    relay_terms(0)
     wait_keys(1, (5, 6, 7))
     first_pass(1, 5, 8)
-    make_transposed(1)
-    finish_queries(0)
+    stats(1, between)
+    all_second(1)
     finish_terms(0)
     dk_ref[0, 0] = acc_own[0, 0]
     dv_ref[0, 0] = acc_own[0, 1]
@@ -403,9 +426,9 @@
     def _():
         carry.start()
 
-    stats(1)
-    all_second(1)
+    query_terms(1)
     relay_terms(1)
+    finish_queries(0)
     finish_queries(1)
     finish_terms(1)
 
@@ -430,7 +453,8 @@
 
 
 def body(queries, out_grad, keys, values, entering_keys, entering_values, key_grads_in, value_grads_in, group_order, *, sections):
-    any_spec = pl.BlockSpec(memory_space=pl.ANY)
+    arrays = (queries, out_grad, keys, values, entering_keys, entering_values, key_grads_in, value_grads_in)
+    any_spec = pl.BlockSpec(memory_space=pltpu.HBM)
     vmem = pl.BlockSpec(memory_space=pltpu.VMEM)
     total = 2 * HEADS * ROWS
     bf16, f32 = jnp.bfloat16, jnp.float32
@@ -449,17 +473,17 @@
             pltpu.VMEM((2, 2, HEADS, ROWS, DIM), bf16),
             pltpu.VMEM((2, CHIPS * ROWS, DIM), bf16),
             pltpu.VMEM((2, CHIPS * ROWS, DIM), bf16),
-            pltpu.VMEM((DIM, CHIPS * ROWS), bf16),
-            pltpu.VMEM((CHIPS * ROWS, total), f32),
-            pltpu.VMEM((CHIPS * ROWS, total), f32),
-            pltpu.VMEM((CHIPS, total), f32),
-            pltpu.VMEM((CHIPS, total), f32),
-            pltpu.VMEM((CHIPS, total), f32),
+            pltpu.VMEM((2, DIM, CHIPS * ROWS), bf16),
+            pltpu.VMEM((2, CHIPS * ROWS, total), f32),
+            pltpu.VMEM((2, CHIPS * ROWS, total), f32),
+            pltpu.VMEM((2, CHIPS, total), f32),
+            pltpu.VMEM((2, CHIPS, total), f32),
+            pltpu.VMEM((2, CHIPS, total), f32),
             pltpu.VMEM((2, CHIPS, total), f32),
             pltpu.VMEM((2, 8, total), f32),
             pltpu.VMEM((2, 8, total), f32),
             pltpu.VMEM((3 * ROWS, WIDE), bf16),
-            pltpu.VMEM((3 * ROWS, WIDE), bf16),
+            pltpu.VMEM((CHIPS * ROWS, total), bf16),
             pltpu.VMEM((2, 3 * ROWS, DIM), f32),
             pltpu.VMEM((2, DIM, total), f32),
             pltpu.VMEM((2, DIM, total // 2), f32),
@@ -487,9 +511,9 @@
             dma((2,)),
         ],
         compiler_params=pltpu.CompilerParams(
-            collective_id=0, has_side_effects=True, vmem_limit_bytes=60 << 20
+            collective_id=0, has_side_effects=True, vmem_limit_bytes=49 << 20
         ),
-    )(group_order, queries, out_grad, keys, values, entering_keys, entering_values, key_grads_in, value_grads_in)
+    )(group_order, *(pltpu.with_memory_space_constraint(x, pltpu.HBM) for x in arrays))
 
 
 def solution(mesh):

time: 63.4 us -> 50.7 us (0.80)
  Pallas kernels: 59.1 us -> 46.7 us
  local copies, waits for them, and re-layouts: 3.51 us -> 2.75 us
    pallas_call x1, Pallas kernels: 59.1 us -> 46.7 us  [body(): pl.pallas_call(functools.partial(kernel, sections), out_shape=(jax.ShapeD...]
    unnamed x7 -> x5, local copies, waits for them, and re-layouts: 3.51 us -> 2.75 us
where the time goes in v3:
time: 50.7 us; the launch traced here: 50.1 us
  Pallas kernels  46.7 us (92%)
  local copies, waits for them, and re-layouts  2.75 us (5%)
  between operations  0.65 us (1%)
    pallas_call x1, Pallas kernels, body(): pl.pallas_call(functools.partial(kernel, sections), out_shape=(jax.ShapeD...  46.7 us
    unnamed x5, local copies, waits for them, and re-layouts  2.75 us

profile of v3, /device:TPU:1, one launch (start us, length us, event | category | flops | bytes accessed | tf_op | source)
XLA Modules:
  0.0 50.1 jit_solution(10758457822251311656)
XLA Ops:
  0.6 0.0 copy-start
  0.6 0.6 %copy-done = s32[16]{0:T(128)S(1)} copy-done((s32[16]{0:T(128)S(1)}, s32[16]{0:T(128)}, u32[]{:S(2)}) %copy-start) | copy-done | bytes 88
  1.3 46.7 %shard_map.112 = (bf16[2,1,128,1024]{3,2,1,0:T(8,128)(2,1)S(1)}, f32[2,1,128,128]{3,2,1,0:T(8,128)S(1)}, f32[2,1,128,128]{3,2,1,0:T(8,128)S(1)}) custom-call(s32[16]{0:T(128)S(1)} %copy-done, bf16[2,1,128,1024]{3,2,1,0:T(8,128)(2,1)} %q_ref.1, bf16[2,1,128,1024]{3,2,1,0:T(8,128)(2,1)} %g_ref.1, bf16[1,128,128]{2,1,0:T(8,128)(2,1)} %k_ref.1, ...), custom_call_target="tpu_custom_call" | custom-call | tf_op jit(solution)/shard_map/pallas_call | solution.py:462
  48.0 0.8 %copy.15 = bf16[2,1,128,1024]{3,2,1,0:T(8,128)(2,1)} copy(bf16[2,1,128,1024]{3,2,1,0:T(8,128)(2,1)S(1)} %get-tuple-element.6) | data formatting | bytes 1048576
  48.8 0.7 %copy.16 = f32[2,1,128,128]{3,2,1,0:T(8,128)} copy(f32[2,1,128,128]{3,2,1,0:T(8,128)S(1)} %get-tuple-element.7) | data formatting | bytes 262144
  49.4 0.7 %copy.17 = f32[2,1,128,128]{3,2,1,0:T(8,128)} copy(f32[2,1,128,128]{3,2,1,0:T(8,128)S(1)} %get-tuple-element.8) | data formatting | bytes 262144
Async XLA Ops:
  0.6 0.7 %copy-start = (s32[16]{0:T(128)S(1)}, s32[16]{0:T(128)}, u32[]{:S(2)}) copy-start(s32[16]{0:T(128)} %order_ref.1) | copy-start | bytes 196

commit v4 on v3

--- a/solution.py
+++ b/solution.py
@@ -13,8 +13,8 @@
 ROWS = 128
 CHUNK = 256
 WIDE = 512
-UNROLL = 2
-UNROLL2 = 2
+UNROLL = 4
+UNROLL2 = 4
 NEG = -1e30
 MESH = pl.DeviceIdType.MESH
 SCALE = 1.0 / math.sqrt(DIM)
@@ -30,6 +30,7 @@
 OFFSETS = (0, 1, -1, 2, -2, 3, -3, 4)
 CHIPS = len(OFFSETS)
 NEAR = (3, 4, 1, 2)
+TERMS = (((5, 8), (0, 3), (3, 5)), ((7, 8), (5, 7), (0, 3), (3, 5)))
 
 
 def kernel(
@@ -181,11 +182,9 @@
 
     gather[1][0] = shift_keys(k_ref.at[0], v_ref.at[0])
 
-    def start_next_gather():
-        for cp in gather[1][0]:
-            cp.wait_recv()
+    def start_next_gather(ps):
         rows = pl.ds(0, ROWS)
-        for p in NEAR:
+        for p in ps:
             gather[1][p] = kv_copies(1, p, peer(sec, OFFSETS[p]), kb.at[1, rows], vb.at[1, rows])
             for cp in gather[1][p]:
                 cp.start()
@@ -384,32 +383,37 @@
             cp.wait_recv()
 
     def all_second(t):
-        for a, b in ((5, 8), (0, 3), (3, 5)):
+        for a, b in TERMS[t]:
             second_pass(t, a, b)
             send_terms(t, a, b)
 
     def ahead():
         make_transposed(0, (5, 6, 7))
         relay_gather(1)
-        wait_keys(1, (1, 2))
-        first_pass(1, 1, 5)
+        first_pass(1, 3, 5)
 
     def between():
         relay_terms(0)
         query_terms(0)
-        make_transposed(1, range(1, CHIPS))
+        make_transposed(1, range(3, CHIPS))
 
     swap_wait(0)
     first_pass(0, 0, 1)
     make_transposed(0, (0,))
+    for cp in gather[1][0]:
+        cp.wait_recv()
+    start_next_gather((1, 2))
     relay_gather(0)
-    start_next_gather()
+    start_next_gather((3, 4))
     swap_wait(1)
     first_pass(1, 0, 1)
     make_transposed(1, (0,))
     wait_keys(0, (1, 2))
     first_pass(0, 1, 5)
     make_transposed(0, (1, 2, 3, 4))
+    wait_keys(1, (1, 2))
+    first_pass(1, 1, 3)
+    make_transposed(1, (1, 2))
     wait_keys(0, (5, 6, 7))
     first_pass(0, 5, 8)
     stats(0, ahead)
@@ -453,7 +457,7 @@
 
 
 def body(queries, out_grad, keys, values, entering_keys, entering_values, key_grads_in, value_grads_in, group_order, *, sections):
-    arrays = (queries, out_grad, keys, values, entering_keys, entering_values, key_grads_in, value_grads_in)
+    arrays = (group_order, queries, out_grad, keys, values, entering_keys, entering_values, key_grads_in, value_grads_in)
     any_spec = pl.BlockSpec(memory_space=pltpu.HBM)
     vmem = pl.BlockSpec(memory_space=pltpu.VMEM)
     total = 2 * HEADS * ROWS
@@ -513,7 +517,7 @@
         compiler_params=pltpu.CompilerParams(
             collective_id=0, has_side_effects=True, vmem_limit_bytes=49 << 20
         ),
-    )(group_order, *(pltpu.with_memory_space_constraint(x, pltpu.HBM) for x in arrays))
+    )(*(pltpu.with_memory_space_constraint(x, pltpu.HBM) for x in arrays))
 
 
 def solution(mesh):

time: 50.7 us -> 49.1 us (0.968)
  Pallas kernels: 46.7 us -> 45.5 us
  local copies, waits for them, and re-layouts: 2.75 us -> 2.11 us
    pallas_call x1, Pallas kernels: 46.7 us -> 45.5 us  [body(): pl.pallas_call(functools.partial(kernel, sections), out_shape=(jax.ShapeD...]
    unnamed x5 -> x3, local copies, waits for them, and re-layouts: 2.75 us -> 2.11 us
where the time goes in v4:
time: 49.1 us; the launch traced here: 48.2 us
  Pallas kernels  45.5 us (93%)
  local copies, waits for them, and re-layouts  2.11 us (4%)
  between operations  0.64 us (1%)
    pallas_call x1, Pallas kernels, body(): pl.pallas_call(functools.partial(kernel, sections), out_shape=(jax.ShapeD...  45.5 us
    unnamed x3, local copies, waits for them, and re-layouts  2.11 us

profile of v4, /device:TPU:1, one launch (start us, length us, event | category | flops | bytes accessed | tf_op | source)
XLA Modules:
  0.0 48.2 jit_solution(13039082029699527622)
XLA Ops:
  0.6 45.5 %shard_map.112 = (bf16[2,1,128,1024]{3,2,1,0:T(8,128)(2,1)S(1)}, f32[2,1,128,128]{3,2,1,0:T(8,128)S(1)}, f32[2,1,128,128]{3,2,1,0:T(8,128)S(1)}) custom-call(s32[16]{0:T(128)} %order_ref.1, bf16[2,1,128,1024]{3,2,1,0:T(8,128)(2,1)} %q_ref.1, bf16[2,1,128,1024]{3,2,1,0:T(8,128)(2,1)} %g_ref.1, bf16[1,128,128]{2,1,0:T(8,128)(2,1)} %k_ref.1, ...), custom_call_target="tpu_custom_call" | custom-call | tf_op jit(solution)/shard_map/pallas_call | solution.py:466
  46.1 0.8 %copy.15 = bf16[2,1,128,1024]{3,2,1,0:T(8,128)(2,1)} copy(bf16[2,1,128,1024]{3,2,1,0:T(8,128)(2,1)S(1)} %get-tuple-element.6) | data formatting | bytes 1048576
  46.9 0.7 %copy.16 = f32[2,1,128,128]{3,2,1,0:T(8,128)} copy(f32[2,1,128,128]{3,2,1,0:T(8,128)S(1)} %get-tuple-element.7) | data formatting | bytes 262144
  47.6 0.7 %copy.17 = f32[2,1,128,128]{3,2,1,0:T(8,128)} copy(f32[2,1,128,128]{3,2,1,0:T(8,128)S(1)} %get-tuple-element.8) | data formatting | bytes 262144

commit v5 on v4

--- a/solution.py
+++ b/solution.py
@@ -190,18 +190,19 @@
                 cp.start()
 
     def relay_gather(t):
-        for p, near, far in ((3, 1, 5), (4, 2, 6)):
-            for cp in gather[t][p]:
-                cp.wait_recv()
-            rows = pl.ds(p * ROWS, ROWS)
-            k_src, v_src = kb.at[t, rows], vb.at[t, rows]
-            gather[t][far] = kv_copies(t, far, peer(sec, OFFSETS[near]), k_src, v_src)
-            for cp in gather[t][far]:
+        gather[t][7] = []
+        for i in range(2):
+            for p, near, far in ((3, 1, 5), (4, 2, 6)):
+                gather[t][p][i].wait_recv()
+                rows = pl.ds(p * ROWS, ROWS)
+                k_src, v_src = kb.at[t, rows], vb.at[t, rows]
+                cp = kv_copies(t, far, peer(sec, OFFSETS[near]), k_src, v_src)[i]
                 cp.start()
-            half = p - 3
-            cp = kv_copies(t, 7, peer(sec, OFFSETS[p]), k_src, v_src)[half]
-            cp.start()
-            gather[t].setdefault(7, []).append(cp)
+                gather[t].setdefault(far, []).append(cp)
+                if i == p - 3:
+                    cp = kv_copies(t, 7, peer(sec, OFFSETS[p]), k_src, v_src)[i]
+                    cp.start()
+                    gather[t][7].append(cp)
 
     def wait_keys(t, ps):
         for p in ps:
@@ -302,13 +303,13 @@
 
         dq_copies[t].start()
 
-    sends = [[], []]
-    middle = [[], []]
+    sends = [{}, {}]
+    middle = [{}, {}]
 
     def push(t, src, buf, slot, sem_slot, dev, keep):
         cp = remote(src, buf.at[slot], rss.at[t, sem_slot], rsr.at[t, sem_slot], dev)
         cp.start()
-        keep.append(cp)
+        keep[sem_slot] = cp
 
     def send_terms(t, a, b):
         for p in range(a, b):
@@ -334,10 +335,10 @@
                     push(t, rs_out.at[t, p, 1], rs_far, (t, 1), 0, peer(sec, 2), middle[t])
 
     def relay_terms(t):
-        for cp in middle[t]:
-            cp.wait_recv()
         for p in (3, 4):
             n = p - 3
+            for slot in ((5, 7), (6, 0))[n]:
+                middle[t][slot].wait_recv()
             dk = mid_own[n, 0] + rs_mid[t, n, 0].astype(jnp.float32)
             dv = mid_own[n, 1] + rs_mid[t, n, 1].astype(jnp.float32)
             far = rs_far[t, n].astype(jnp.float32)
@@ -362,7 +363,7 @@
             dq_ref[t, 0, :, pl.ds(h * DIM, DIM)] = full.T.astype(jnp.bfloat16)
 
     def finish_terms(t):
-        for cp in sends[t]:
+        for cp in sends[t].values():
             cp.wait_recv()
         for i in range(2):
             s = acc_own[t, i]
@@ -390,30 +391,27 @@
     def ahead():
         make_transposed(0, (5, 6, 7))
         relay_gather(1)
-        first_pass(1, 3, 5)
+        wait_keys(1, (1, 2))
+        first_pass(1, 1, 5)
 
     def between():
         relay_terms(0)
         query_terms(0)
-        make_transposed(1, range(3, CHIPS))
+        make_transposed(1, range(1, CHIPS))
 
     swap_wait(0)
     first_pass(0, 0, 1)
     make_transposed(0, (0,))
+    relay_gather(0)
     for cp in gather[1][0]:
         cp.wait_recv()
-    start_next_gather((1, 2))
-    relay_gather(0)
-    start_next_gather((3, 4))
+    start_next_gather((3, 4, 1, 2))
     swap_wait(1)
     first_pass(1, 0, 1)
     make_transposed(1, (0,))
     wait_keys(0, (1, 2))
     first_pass(0, 1, 5)
     make_transposed(0, (1, 2, 3, 4))
-    wait_keys(1, (1, 2))
-    first_pass(1, 1, 3)
-    make_transposed(1, (1, 2))
     wait_keys(0, (5, 6, 7))
     first_pass(0, 5, 8)
     stats(0, ahead)
@@ -431,8 +429,8 @@
         carry.start()
 
     query_terms(1)
+    finish_queries(0)
     relay_terms(1)
-    finish_queries(0)
     finish_queries(1)
     finish_terms(1)
 
@@ -452,8 +450,19 @@
         for cps in gather[t].values():
             for cp in cps:
                 cp.wait_send()
-        for cp in swaps[t] + middle[t] + sends[t]:
+        for cp in swaps[t] + list(middle[t].values()) + list(sends[t].values()):
             cp.wait_send()
+
+
+def store_results(a, b, c, out_a, out_b, out_c, sems):
+    copies = [
+        pltpu.make_async_copy(src, dst, sems.at[i])
+        for i, (src, dst) in enumerate(((a, out_a), (b, out_b), (c, out_c)))
+    ]
+    for cp in copies:
+        cp.start()
+    for cp in copies:
+        cp.wait()
 
 
 def body(queries, out_grad, keys, values, entering_keys, entering_values, key_grads_in, value_grads_in, group_order, *, sections):
@@ -463,7 +472,7 @@
     total = 2 * HEADS * ROWS
     bf16, f32 = jnp.bfloat16, jnp.float32
     dma = pltpu.SemaphoreType.DMA
-    return pl.pallas_call(
+    results = pl.pallas_call(
         functools.partial(kernel, sections),
         out_shape=(
             jax.ShapeDtypeStruct((2, 1, ROWS, HEADS * DIM), bf16),
@@ -518,6 +527,14 @@
             collective_id=0, has_side_effects=True, vmem_limit_bytes=49 << 20
         ),
     )(*(pltpu.with_memory_space_constraint(x, pltpu.HBM) for x in arrays))
+    return pl.pallas_call(
+        store_results,
+        out_shape=tuple(jax.ShapeDtypeStruct(r.shape, r.dtype) for r in results),
+        in_specs=[pl.BlockSpec(memory_space=pltpu.VMEM)] * 3,
+        out_specs=(pl.BlockSpec(memory_space=pl.ANY),) * 3,
+        scratch_shapes=[dma((3,))],
+        compiler_params=pltpu.CompilerParams(vmem_limit_bytes=4 << 20),
+    )(*results)
 
 
 def solution(mesh):

time: 49.1 us -> 47.7 us (0.971)
  the two profiles are of different devices: /device:TPU:1 before, /device:TPU:32 now
where the time goes in v5:
time: 47.7 us; the launch traced here: 47.6 us
  Pallas kernels  46.9 us (98%)
  between operations  0.64 us (1%)
    pallas_call x1, Pallas kernels, body(): pl.pallas_call(functools.partial(kernel, sections), out_shape=(jax.ShapeD...  46 us

profile of v5, /device:TPU:32, one launch (start us, length us, event | category | flops | bytes accessed | tf_op | source)
XLA Modules:
  0.0 47.6 jit_solution(16146144507623555252)
XLA Ops:
  0.6 46.0 %shard_map.112 = (bf16[2,1,128,1024]{3,2,1,0:T(8,128)(2,1)S(1)}, f32[2,1,128,128]{3,2,1,0:T(8,128)S(1)}, f32[2,1,128,128]{3,2,1,0:T(8,128)S(1)}) custom-call(s32[16]{0:T(128)} %order_ref.1, bf16[2,1,128,1024]{3,2,1,0:T(8,128)(2,1)} %q_ref.1, bf16[2,1,128,1024]{3,2,1,0:T(8,128)(2,1)} %g_ref.1, bf16[1,128,128]{2,1,0:T(8,128)(2,1)} %k_ref.1, ...), custom_call_target="tpu_custom_call" | custom-call | tf_op jit(solution)/shard_map/pallas_call | solution.py:475
  46.7 0.9 %shard_map.113 = (bf16[2,1,128,1024]{3,2,1,0:T(8,128)(2,1)}, f32[2,1,128,128]{3,2,1,0:T(8,128)}, f32[2,1,128,128]{3,2,1,0:T(8,128)}) custom-call(bf16[2,1,128,1024]{3,2,1,0:T(8,128)(2,1)S(1)} %get-tuple-element.6.a, f32[2,1,128,128]{3,2,1,0:T(8,128)S(1)} %get-tuple-element.7.b, f32[2,1,128,128]{3,2,1,0:T(8,128)S(1)} %get-tuple-element.8.c), custom_call_target="tpu_custom_call" | custom-call | tf_op jit(solution)/shard_map/pallas_call | solution.py:530
